TPU v7x, 32 devices: a whole 2x2x4 slice. The times are simulated.
32 devices in a mesh: dp: 2 (over y), row: 4 (over x, core), col: 4 (over z).
Axes of the slice: x: 2, y: 2, z: 4, core: 2. Of those that a mesh axis runs over, the one named last changes fastest.
Arguments:
- grad_out: bfloat16 [512, 8192], P(('dp', 'col'), 'row'), may hold values from -6 to 6
- saved_hidden: bfloat16 [512, 26624], P(('dp', 'row'), 'col'), may hold values from -0.26367188 to 0.26367188
- down_weight: bfloat16 [26624, 8192], P('col', 'row'), may hold values from -0.0625 to 0.0625
Outputs:
- input_grad: bfloat16 [512, 26624], P(('dp', 'row'), 'col')
- weight_grad: bfloat16 [26624, 8192], P(('col', 'dp'), 'row')
All inputs are finite; a program needn't handle non-finite values.
Results may differ from a plain program's by a relative error of at most 0.001.
Values may be sent and summed in bfloat16 or wider, within the bound.
No kernel may reach another device: no remote copies, remote signals or barrier semaphores. Data moves between devices by JAX's collectives and lax.ppermute only.
A program may use at most 128 MiB of HBM per device.

v0:
```python
import functools

import jax
import jax.numpy as jnp
from jax import lax
from jax.experimental import pallas as pl
from jax.experimental.pallas import tpu as pltpu
from jax.sharding import PartitionSpec as P


CORES = 2
LOADS = 3
EARLY = 1
STEPS = (8, 8, 6, 4)
ACROSS = 1
SHARES = (17, 17, 18)
CHUNKS = len(SHARES)
NT = (((1,), (1,)), ((), ()))
TN = (((0,), (0,)), ((), ()))
SMALL = 12 * 2**20
SPLIT = 8
LANES = 128
WIDE_LIMIT = 28 * 2**20
GRAD_MOST = 6.0
WEIGHT_MOST = 0.0625
POWER = 8
TOP = 120.0


def native(grad_out, saved_hidden, down_weight):
    local_rows = saved_hidden.shape[0]
    gathered_all = lax.all_gather(grad_out, ("dp", "col"), axis=0, tiled=True)
    copy_count = lax.axis_size("dp")
    row_count = lax.axis_size("row")
    copy_rows = gathered_all.shape[0] // copy_count
    grad_copy = lax.dynamic_slice_in_dim(
        gathered_all, lax.axis_index("dp") * copy_rows, copy_rows, 0
    )
    hidden_parts = lax.all_to_all(saved_hidden, "dp", split_axis=1, concat_axis=0, tiled=True)
    hidden_stack = lax.all_gather(hidden_parts, "row", axis=0, tiled=True)
    hidden_grid = hidden_stack.reshape(row_count, copy_count, local_rows, hidden_stack.shape[1])
    grad_grid = gathered_all.reshape(copy_count, row_count, local_rows, gathered_all.shape[1])
    weight_grad = jnp.einsum(
        "rdtk,drtn->kn", hidden_grid, grad_grid, preferred_element_type=jnp.float32
    )
    input_grad = lax.psum_scatter(
        lax.dot_general(
            grad_copy, down_weight, (((1,), (1,)), ((), ())), preferred_element_type=jnp.float32
        ),
        "row",
        scatter_dimension=0,
        tiled=True,
    )
    return (input_grad.astype(jnp.bfloat16), weight_grad.astype(jnp.bfloat16))


def encode(value, scale):
    scaled = value * scale
    square = scaled * scaled
    fourth = square * square
    eighth = fourth * fourth
    return jnp.where(scaled < 0, -eighth, eighth).astype(jnp.bfloat16)


def decode(code, scale):
    wide = code.astype(jnp.float32)
    half = lax.rsqrt(jnp.maximum(jnp.abs(wide), 2.0**-126))
    fourth = lax.rsqrt(half)
    root = fourth * lax.rsqrt(fourth) * (1.0 / scale)
    return jnp.where(wide < 0, -root, jnp.where(wide > 0, root, 0.0))


def swap(x, axis, mask):
    n = lax.axis_size(axis)
    return lax.ppermute(x, axis, [(i, i ^ mask) for i in range(n)])


def put_blocks(at, blocks, held):
    rows = blocks[0].shape[0]
    for i, block in enumerate(blocks):
        held[pl.ds(pl.multiple_of(at[i] * rows, rows), rows), :] = block[...]


def start_loads(spans, w, outs, sem):
    copies = []
    for (lo, hi), out in zip(spans, outs):
        step = (hi - lo) // SPLIT
        for i in range(SPLIT):
            part = w.at[pl.ds(lo + i * step, step)]
            copies.append(pltpu.make_async_copy(part, out.at[pl.ds(i * step, step)], sem.at[len(copies)]))
    for c in copies:
        c.start()
    return copies


def load_kernel(spans, at, w, *refs):
    del at
    for c in start_loads(spans, w, refs[:-1], refs[-1]):
        c.wait()


def load(at, weight, spans):
    depth = weight.shape[1]
    return pl.pallas_call(
        functools.partial(load_kernel, spans),
        in_specs=[pl.BlockSpec(memory_space=pltpu.SMEM), pl.BlockSpec(memory_space=pltpu.HBM)],
        out_specs=[pl.BlockSpec(memory_space=pltpu.VMEM)] * len(spans),
        out_shape=[pltpu.VMEM((hi - lo, depth), weight.dtype) for lo, hi in spans],
        scratch_shapes=[pltpu.SemaphoreType.DMA((SPLIT * len(spans),))],
        cost_estimate=pl.CostEstimate(
            flops=0, bytes_accessed=2 * depth * sum(hi - lo for lo, hi in spans), transcendentals=0
        ),
        compiler_params=pltpu.CompilerParams(vmem_limit_bytes=SMALL),
    )(at, pltpu.with_memory_space_constraint(weight, pltpu.HBM))


def product_kernel(n_block, spans, *refs):
    if n_block:
        at, refs = refs[0], refs[1:]
    n = max(n_block, 1)
    blocks, now, refs = refs[:n], refs[n : n + len(spans)], refs[n + len(spans) :]
    keep, give = refs[:2]
    held = blocks[0]
    if n_block:
        held = refs[2]
        put_blocks(at, blocks, held)
    top = keep.shape[0]
    lo = 0
    for ref, (first, last) in zip(now, spans):
        hi = lo + last - first
        part = lax.dot_general(
            held[...], ref[first:last, :], NT, preferred_element_type=jnp.float32
        )
        keep[:, lo:hi] = part[:top]
        give[:, lo:hi] = part[top:]
        lo = hi


def product(grads, now):
    at, blocks = grads if isinstance(grads, tuple) else (None, [])
    rows = 4 * blocks[0].shape[0] if blocks else grads.shape[0]
    depth = now[0][2].shape[1]
    spans = [(first, last) for first, last, _ in now]
    tall = sum(last - first for first, last in spans)
    whole = pl.BlockSpec(memory_space=pltpu.VMEM)
    outs = pl.pallas_call(
        functools.partial(product_kernel, len(blocks), spans),
        in_specs=[pl.BlockSpec(memory_space=pltpu.SMEM)] * (at is not None)
        + [whole] * (max(len(blocks), 1) + len(now)),
        out_specs=[whole] * (2 + (at is not None)),
        out_shape=[jax.ShapeDtypeStruct((rows // 2, tall), jnp.float32)] * 2
        + [pltpu.VMEM((rows, depth), now[0][2].dtype)] * (at is not None),
        cost_estimate=pl.CostEstimate(
            flops=2 * rows * tall * depth, bytes_accessed=2 * tall * depth, transcendentals=0
        ),
        compiler_params=pltpu.CompilerParams(vmem_limit_bytes=SMALL),
    )(
        *([] if at is None else [at]),
        *(blocks or [grads]),
        *[pltpu.with_memory_space_constraint(w, pltpu.VMEM) for _, _, w in now],
    )
    return outs[0], outs[1], outs[-1] if blocks else grads


def finish_kernel(scale, ready, *refs):
    done, refs, (out, staged, sem) = refs[:ready], refs[ready:-3], refs[-3:]
    rows = out.shape[0]
    copies = []
    lo = 0

    def write(tall):
        window = pl.ds(lo, tall)
        copies.append(
            pltpu.make_async_copy(staged.at[:, window], out.at[:, window], sem.at[len(copies)])
        )
        copies[-1].start()

    for chunk in done:
        tall = chunk.shape[1]
        staged[:, lo : lo + tall] = chunk[...]
        write(tall)
        lo += tall
    for keep, got, far in zip(refs[0::3], refs[1::3], refs[2::3]):
        tall = far.shape[1]
        value = (keep[:rows] + got[:rows]) + decode(far[...], scale)
        staged[:, lo : lo + tall] = value.astype(staged.dtype)
        write(tall)
        lo += tall
    for c in copies:
        c.wait()


def finish(done, parts, scale, dtype):
    rows = parts[0][2].shape[0]
    whole = pl.BlockSpec(memory_space=pltpu.VMEM)
    hid = sum(c.shape[1] for c in done) + sum(p[2].shape[1] for p in parts)
    return pl.pallas_call(
        functools.partial(finish_kernel, scale, len(done)),
        in_specs=[whole] * (len(done) + 3 * len(parts)),
        out_specs=pl.BlockSpec(memory_space=pltpu.HBM),
        out_shape=jax.ShapeDtypeStruct((rows, hid), dtype),
        scratch_shapes=[
            pltpu.VMEM((rows, hid), dtype),
            pltpu.SemaphoreType.DMA((len(done) + len(parts),)),
        ],
        cost_estimate=pl.CostEstimate(
            flops=20 * rows * hid, bytes_accessed=14 * rows * hid, transcendentals=0
        ),
        compiler_params=pltpu.CompilerParams(vmem_limit_bytes=SMALL),
    )(*done, *[x for p in parts for x in p])


def early_kernel(scale, keep, got, far, out):
    rows = out.shape[0]
    out[...] = ((keep[:rows] + got[:rows]) + decode(far[...], scale)).astype(out.dtype)


def early(part, scale, dtype):
    rows, tall = part[2].shape
    whole = pl.BlockSpec(memory_space=pltpu.VMEM)
    return pl.pallas_call(
        functools.partial(early_kernel, scale),
        in_specs=[whole] * 3,
        out_specs=whole,
        out_shape=pltpu.VMEM((rows, tall), dtype),
        cost_estimate=pl.CostEstimate(
            flops=20 * rows * tall, bytes_accessed=14 * rows * tall, transcendentals=0
        ),
        compiler_params=pltpu.CompilerParams(vmem_limit_bytes=SMALL),
    )(*part)


def weight_kernel(n_hid, pieces, at, *refs):
    rows = refs[0].shape[0]
    hidden, own, peers = refs[:n_hid], refs[n_hid], refs[n_hid + 1 : -4]
    out, held, slots, sem = refs[-4:]
    half = own.shape[0]
    held[:half, :] = own[...]
    for peer, places in zip(peers, ((0, 2), (1,), (3,))):
        for i, place in enumerate(places):
            start = pl.multiple_of(half + at[place] * rows, rows)
            held[pl.ds(start, rows), :] = peer[i * rows : (i + 1) * rows]
    copies = []
    for n, (top, end, lo, hi) in enumerate(pieces):
        if n >= 2:
            copies[n - 2].wait()
        stacked = jnp.concatenate([h[:, top:end] for h in hidden])
        slot = slots.at[n % 2, : end - top, : hi - lo]
        slot[...] = lax.dot_general(
            stacked, held[:, lo:hi], TN, preferred_element_type=jnp.float32
        ).astype(out.dtype)
        place = out.at[pl.ds(top, end - top), pl.ds(lo, hi - lo)]
        copies.append(pltpu.make_async_copy(slot, place, sem.at[n]))
        copies[-1].start()
    for c in copies[-2:]:
        c.wait()


def weight_product(at, hidden, own, peers):
    rows, hid = hidden[0].shape
    depth = own.shape[1]
    tokens = rows * len(hidden)
    tiles = hid // LANES
    edges = [LANES * (tiles * sum(STEPS[:i]) // sum(STEPS)) for i in range(len(STEPS) + 1)]
    pieces = [(top, end, lo, lo + depth // ACROSS) for top, end in zip(edges, edges[1:]) for lo in range(0, depth, depth // ACROSS)]
    tall, wide = max(end - top for top, end, _, _ in pieces), depth // ACROSS
    whole = pl.BlockSpec(memory_space=pltpu.VMEM)
    return pl.pallas_call(
        functools.partial(weight_kernel, len(hidden), pieces),
        in_specs=[pl.BlockSpec(memory_space=pltpu.SMEM)] + [whole] * (len(hidden) + 1 + len(peers)),
        out_specs=pl.BlockSpec(memory_space=pltpu.HBM),
        out_shape=jax.ShapeDtypeStruct((hid, depth), hidden[0].dtype),
        scratch_shapes=[
            pltpu.VMEM((tokens, depth), hidden[0].dtype),
            pltpu.VMEM((2, tall, wide), hidden[0].dtype),
            pltpu.SemaphoreType.DMA((len(pieces),)),
        ],
        cost_estimate=pl.CostEstimate(
            flops=2 * tokens * hid * depth, bytes_accessed=2 * hid * depth, transcendentals=0
        ),
        compiler_params=pltpu.CompilerParams(vmem_limit_bytes=WIDE_LIMIT),
    )(at, *hidden, own, *peers)


def paired(grad_out, saved_hidden, down_weight):
    d, r, z = (lax.axis_index(a) for a in ("dp", "row", "col"))
    chip = CORES
    rows = saved_hidden.shape[0]
    hid, depth = down_weight.shape
    half = hid // 2

    pair = swap(grad_out, "col", 1)
    rev = swap(grad_out, "col", 3)
    s2 = swap(rev, "col", 1)
    two = jnp.concatenate([grad_out, rev])
    y_two = swap(two, "dp", 1)
    y_pair = swap(pair, "dp", 1)
    y_rev = y_two[grad_out.shape[0] :]
    y_s2 = swap(y_rev, "col", 1)
    h_give = lax.dynamic_slice_in_dim(saved_hidden, (1 - d) * half, half, 1)
    h_mine = lax.dynamic_slice_in_dim(saved_hidden, d * half, half, 1)
    h_peer = swap(h_give, "dp", 1)
    h_far = swap(h_mine, "row", chip)
    h_peer_far = swap(h_peer, "row", chip)
    mine = [h_mine, h_peer, h_far, h_peer_far]
    mate = [swap(h, "row", 1) for h in mine]

    ks = [r ^ z ^ m for m in (0, 1, 3, 2)]
    at = jnp.stack([((k & 1) << 1) | (k >> 1) for k in ks]).astype(jnp.int32)
    scale = 2.0 ** (TOP / POWER) / (CORES * depth * GRAD_MOST * WEIGHT_MOST)
    tiles = hid // LANES
    edges = [LANES * (tiles * sum(SHARES[:i]) // sum(SHARES)) for i in range(CHUNKS + 1)]
    cuts = [LANES * (tiles * i // LOADS) for i in range(LOADS + 1)]
    loaded = []
    for lo, hi in zip(cuts, cuts[1:]):
        (part,) = load(at, down_weight, [(lo, hi)])
        loaded.append((lo, hi, part))
    grads = (at, [grad_out, pair, rev, s2])
    parts = []
    for lo, hi in zip(edges, edges[1:]):
        now = [(max(lo, a) - a, min(hi, b) - a, w) for a, b, w in loaded if a < hi and lo < b]
        keep, give, grads = product(grads, now)
        got = swap(give, "row", 1)
        sent = encode(keep[rows:] + got[rows:], scale)
        parts.append((keep, got, swap(sent, "row", chip)))
    done = [early(part, scale, saved_hidden.dtype) for part in parts[:EARLY]]
    input_grad = finish(done, parts[EARLY:], scale, saved_hidden.dtype)
    weight_grad = weight_product(
        at,
        [mine[0], mine[2], mate[0], mate[2], mine[1], mine[3], mate[1], mate[3]],
        grads,
        [y_two, y_pair, y_s2],
    )
    return input_grad, weight_grad


def local(grad_out, saved_hidden, down_weight):
    sizes = [lax.axis_size(a) for a in ("dp", "row", "col")]
    if sizes[0] == 2 and sizes[1] == 2 * CORES and sizes[2] == sizes[1]:
        return paired(grad_out, saved_hidden, down_weight)
    return native(grad_out, saved_hidden, down_weight)


def solution(mesh):
    placed = (P(("dp", "col"), "row"), P(("dp", "row"), "col"), P("col", "row"))
    return jax.shard_map(
        local,
        mesh=mesh,
        in_specs=placed,
        out_specs=(P(("dp", "row"), "col"), P(("col", "dp"), "row")),
        check_vma=False,
    )
```

profile of v0, /device:TPU:0, one launch (start us, length us, event | category | flops | bytes accessed | tf_op | source)
XLA Modules:
  0.0 100.6 jit_solution(13869619269179693651)
XLA Ops:
  0.6 5.1 %collective-permute-start.1 = (bf16[64,2048]{1,0:T(8,128)(2,1)}, bf16[64,2048]{1,0:T(8,128)(2,1)S(1)}, u32[]{:S(2)}, u32[]{:S(2)}) collective-permute-start(bf16[64,2048]{1,0:T(8,128)(2,1)} %refs_1_.1), channel_id=1, source_target_pairs={{0,3},{1,2},{2,1},{3,0},{4,7},{5,6},{6,5},{7,4},{8,11},{9,10},{10,... | collective-permute-start | bytes 786440 | tf_op jit(solution)/shard_map/ppermute | solution.py:75
  5.8 7.5 %collective-permute-done.1.refs_3_ = bf16[64,2048]{1,0:T(8,128)(2,1)S(1)} collective-permute-done((bf16[64,2048]{1,0:T(8,128)(2,1)}, bf16[64,2048]{1,0:T(8,128)(2,1)S(1)}, u32[]{:S(2)}, u32[]{:S(2)}) %collective-permute-start.1) | collective-permute-done | bytes 262176 | tf_op jit(solution)/shard_map/ppermute | solution.py:75
  13.2 4.4 %collective-permute-start.2 = (bf16[64,2048]{1,0:T(8,128)(2,1)S(1)}, bf16[64,2048]{1,0:T(8,128)(2,1)S(1)}, u32[]{:S(2)}, u32[]{:S(2)}) collective-permute-start(bf16[64,2048]{1,0:T(8,128)(2,1)S(1)} %collective-permute-done.1.refs_3_), channel_id=1, source_target_pairs={{0,1},{1,0},{2,3},{3,2},{4,5},{5,4},{6,7},{7,6},{8,9},{9,8},{10,11... | collective-permute-start | bytes 786440 | tf_op jit(solution)/shard_map/ppermute | solution.py:75
  17.7 4.2 %shard_map.50.refs_5_ = bf16[2176,2048]{1,0:T(8,128)(2,1)S(1)} custom-call(s32[4]{0:T(128)S(1)} %pad_add_fusion.at.refs_0_, bf16[6656,2048]{1,0:T(8,128)(2,1)} %w.5), custom_call_target="tpu_custom_call" | custom-call | bytes 8912896 | tf_op jit(solution)/shard_map/pallas_call | solution.py:104
  21.9 3.6 %copy-done.2 = bf16[2176,2048]{1,0:T(8,128)(2,1)} copy-done((bf16[2176,2048]{1,0:T(8,128)(2,1)}, bf16[2176,2048]{1,0:T(8,128)(2,1)S(1)}, u32[]{:S(2)}) %copy-start.2) | copy-done | bytes 8912920
  25.4 4.2 %shard_map.53.refs_1_ = bf16[2176,2048]{1,0:T(8,128)(2,1)S(1)} custom-call(s32[4]{0:T(128)S(1)} %pad_add_fusion.at.refs_0_, bf16[6656,2048]{1,0:T(8,128)(2,1)} %w.5), custom_call_target="tpu_custom_call" | custom-call | bytes 8912896 | tf_op jit(solution)/shard_map/pallas_call | solution.py:104
  29.6 3.5 %copy-done = bf16[2176,2048]{1,0:T(8,128)(2,1)} copy-done((bf16[2176,2048]{1,0:T(8,128)(2,1)}, bf16[2176,2048]{1,0:T(8,128)(2,1)S(1)}, u32[]{:S(2)}) %copy-start) | copy-done | bytes 8912920
  33.1 3.5 %copy-done.3 = bf16[2176,2048]{1,0:T(8,128)(2,1)S(1)} copy-done((bf16[2176,2048]{1,0:T(8,128)(2,1)S(1)}, bf16[2176,2048]{1,0:T(8,128)(2,1)}, u32[]{:S(2)}) %copy-start.3) | copy-done | bytes 8912920
  36.6 3.2 %shard_map.51 = (f32[128,2176]{1,0:T(8,128)S(1)}, f32[128,2176]{1,0:T(8,128)S(1)}, bf16[256,2048]{1,0:T(8,128)(2,1)S(1)}) custom-call(s32[4]{0:T(128)S(1)} %pad_add_fusion.at.refs_0_, bf16[64,2048]{1,0:T(8,128)(2,1)S(1)} %copy-done.4, bf16[64,2048]{1,0:T(8,128)(2,1)S(1)} %collective-permute-done.refs_2_, ...), custom_call_target="tpu_custom_call" | custom-call | flops 2281701376 | bytes 8912896 | tf_op jit(solution)/shard_map/pallas_call | solution.py:146
  40.0 1.6 %collective-permute-start.16 = (bf16[128,2048]{1,0:T(8,128)(2,1)S(1)}, bf16[128,2048]{1,0:T(8,128)(2,1)S(1)}, u32[]{:S(2)}, u32[]{:S(2)}) collective-permute-start(bf16[128,2048]{1,0:T(8,128)(2,1)S(1)} %pad_maximum_fusion), channel_id=1, source_target_pairs={{0,16},{16,0},{1,17},{17,1},{2,18},{18,2},{3,19},{19,3},{4,20},{20... | collective-permute-start | bytes 1572872 | tf_op jit(solution)/shard_map/ppermute | solution.py:75
  41.6 2.6 %shard_map.54 = (f32[128,2176]{1,0:T(8,128)S(1)}, f32[128,2176]{1,0:T(8,128)S(1)}) custom-call(bf16[256,2048]{1,0:T(8,128)(2,1)S(1)} %get-tuple-element.11.refs_0_.refs_8_, bf16[2176,2048]{1,0:T(8,128)(2,1)S(1)} %copy-done.1), custom_call_target="tpu_custom_call" | custom-call | flops 2281701376 | bytes 8912896 | tf_op jit(solution)/shard_map/pallas_call | solution.py:146
  44.2 0.3 collective-permute-start.5
  44.5 1.6 %collective-permute-start.9 = (bf16[64,3328]{1,0:T(8,128)(2,1)S(1)}, bf16[64,3328]{1,0:T(8,128)(2,1)S(1)}, u32[]{:S(2)}, u32[]{:S(2)}) collective-permute-start(bf16[64,3328]{1,0:T(8,128)(2,1)S(1)} %get-tuple-element.17.refs_0_), channel_id=1, source_target_pairs={{0,8},{4,12},{8,0},{12,4},{1,9},{5,13},{9,1},{13,5},{2,10},{6,14},... | collective-permute-start | bytes 1277960 | tf_op jit(solution)/shard_map/ppermute | solution.py:75
  46.1 4.3 %shard_map.55.refs_1_ = bf16[2304,2048]{1,0:T(8,128)(2,1)S(1)} custom-call(s32[4]{0:T(128)S(1)} %pad_add_fusion.at.refs_0_, bf16[6656,2048]{1,0:T(8,128)(2,1)} %w.5), custom_call_target="tpu_custom_call" | custom-call | bytes 9437184 | tf_op jit(solution)/shard_map/pallas_call | solution.py:104
  50.5 2.7 %shard_map.56 = (f32[128,2304]{1,0:T(8,128)S(1)}, f32[128,2304]{1,0:T(8,128)S(1)}) custom-call(bf16[256,2048]{1,0:T(8,128)(2,1)S(1)} %get-tuple-element.11.refs_0_.refs_8_, bf16[2304,2048]{1,0:T(8,128)(2,1)S(1)} %shard_map.55.refs_1_), custom_call_target="tpu_custom_call" | custom-call | flops 2415919104 | bytes 9437184 | tf_op jit(solution)/shard_map/pallas_call | solution.py:146
  53.1 1.2 %collective-permute-done.16.refs_9_ = bf16[128,2048]{1,0:T(8,128)(2,1)S(1)} collective-permute-done((bf16[128,2048]{1,0:T(8,128)(2,1)S(1)}, bf16[128,2048]{1,0:T(8,128)(2,1)S(1)}, u32[]{:S(2)}, u32[]{:S(2)}) %collective-permute-start.16) | collective-permute-done | bytes 524320 | tf_op jit(solution)/shard_map/ppermute | solution.py:75
  54.4 1.5 %collective-permute-start.12 = (bf16[64,3328]{1,0:T(8,128)(2,1)S(1)}, bf16[64,3328]{1,0:T(8,128)(2,1)S(1)}, u32[]{:S(2)}, u32[]{:S(2)}) collective-permute-start(bf16[64,3328]{1,0:T(8,128)(2,1)S(1)} %get-tuple-element.16), channel_id=1, source_target_pairs={{0,16},{16,0},{1,17},{17,1},{2,18},{18,2},{3,19},{19,3},{4,20},{20... | collective-permute-start | bytes 1277960 | tf_op jit(solution)/shard_map/ppermute | solution.py:75
  56.0 0.2 fusion.2
  56.2 9.6 %collective-permute-done.12.refs_4_ = bf16[64,3328]{1,0:T(8,128)(2,1)S(1)} collective-permute-done((bf16[64,3328]{1,0:T(8,128)(2,1)S(1)}, bf16[64,3328]{1,0:T(8,128)(2,1)S(1)}, u32[]{:S(2)}, u32[]{:S(2)}) %collective-permute-start.12) | collective-permute-done | bytes 426016 | tf_op jit(solution)/shard_map/ppermute | solution.py:75
  65.7 1.5 %collective-permute-start.17 = (bf16[64,2048]{1,0:T(8,128)(2,1)S(1)}, bf16[64,2048]{1,0:T(8,128)(2,1)S(1)}, u32[]{:S(2)}, u32[]{:S(2)}) collective-permute-start(bf16[64,2048]{1,0:T(8,128)(2,1)S(1)} %collective-permute-done.refs_2_), channel_id=1, source_target_pairs={{0,16},{16,0},{1,17},{17,1},{2,18},{18,2},{3,19},{19,3},{4,20},{20... | collective-permute-start | bytes 786440 | tf_op jit(solution)/shard_map/ppermute | solution.py:75
  67.2 1.5 %collective-permute-start.13 = (bf16[64,3328]{1,0:T(8,128)(2,1)S(1)}, bf16[64,3328]{1,0:T(8,128)(2,1)S(1)}, u32[]{:S(2)}, u32[]{:S(2)}) collective-permute-start(bf16[64,3328]{1,0:T(8,128)(2,1)S(1)} %collective-permute-done.12.refs_4_), channel_id=1, source_target_pairs={{0,8},{4,12},{8,0},{12,4},{1,9},{5,13},{9,1},{13,5},{2,10},{6,14},... | collective-permute-start | bytes 1277960 | tf_op jit(solution)/shard_map/ppermute | solution.py:75
  69.0 0.5 collective-permute-start.11
  69.5 8.0 %collective-permute-done.13.refs_5_ = bf16[64,3328]{1,0:T(8,128)(2,1)S(1)} collective-permute-done((bf16[64,3328]{1,0:T(8,128)(2,1)S(1)}, bf16[64,3328]{1,0:T(8,128)(2,1)S(1)}, u32[]{:S(2)}, u32[]{:S(2)}) %collective-permute-start.13) | collective-permute-done | bytes 426016 | tf_op jit(solution)/shard_map/ppermute | solution.py:75
  77.5 0.2 fusion
  77.7 1.6 %collective-permute-start.4 = (bf16[64,2176]{1,0:T(8,128)(2,1)S(1)}, bf16[64,2176]{1,0:T(8,128)(2,1)S(1)}, u32[]{:S(2)}, u32[]{:S(2)}) collective-permute-start(bf16[64,2176]{1,0:T(8,128)(2,1)S(1)} %fusion.2), channel_id=1, source_target_pairs={{0,8},{4,12},{8,0},{12,4},{1,9},{5,13},{9,1},{13,5},{2,10},{6,14},... | collective-permute-start | bytes 835592 | tf_op jit(solution)/shard_map/ppermute | solution.py:75
  79.2 0.5 collective-permute-start.6
  79.8 1.5 %collective-permute-start.8 = (bf16[64,2304]{1,0:T(8,128)(2,1)S(1)}, bf16[64,2304]{1,0:T(8,128)(2,1)S(1)}, u32[]{:S(2)}, u32[]{:S(2)}) collective-permute-start(bf16[64,2304]{1,0:T(8,128)(2,1)S(1)} %fusion), channel_id=1, source_target_pairs={{0,8},{4,12},{8,0},{12,4},{1,9},{5,13},{9,1},{13,5},{2,10},{6,14},... | collective-permute-start | bytes 884744 | tf_op jit(solution)/shard_map/ppermute | solution.py:75
  81.3 2.6 %collective-permute-done.18.refs_11_ = bf16[64,2048]{1,0:T(8,128)(2,1)S(1)} collective-permute-done((bf16[64,2048]{1,0:T(8,128)(2,1)S(1)}, bf16[64,2048]{1,0:T(8,128)(2,1)S(1)}, u32[]{:S(2)}, u32[]{:S(2)}) %collective-permute-start.18) | collective-permute-done | bytes 262176 | tf_op jit(solution)/shard_map/ppermute | solution.py:75
  83.8 10.0 %shard_map.58 = bf16[3328,2048]{1,0:T(8,128)(2,1)} custom-call(s32[4]{0:T(128)S(1)} %pad_add_fusion.at.refs_0_, bf16[64,3328]{1,0:T(8,128)(2,1)S(1)} %get-tuple-element.17.refs_0_, bf16[64,3328]{1,0:T(8,128)(2,1)S(1)} %collective-permute-done.9.refs_1_, bf16[64,3328]{1,0:T(8,128)(2,1)S(1)} %collective-permute-done.10.refs_2_, ...), custom_call_target="tpu_custom_call" | custom-call | flops 6979321856 | bytes 13631488 | tf_op jit(solution)/shard_map/pallas_call | solution.py:268
  93.9 0.3 shard_map.52.refs_0_
  94.2 4.9 %collective-permute-done.8.refs_6_ = bf16[64,2304]{1,0:T(8,128)(2,1)S(1)} collective-permute-done((bf16[64,2304]{1,0:T(8,128)(2,1)S(1)}, bf16[64,2304]{1,0:T(8,128)(2,1)S(1)}, u32[]{:S(2)}, u32[]{:S(2)}) %collective-permute-start.8) | collective-permute-done | bytes 294944 | tf_op jit(solution)/shard_map/ppermute | solution.py:75
  99.1 1.3 %shard_map.57 = bf16[64,6656]{1,0:T(8,128)(2,1)} custom-call(bf16[64,2176]{1,0:T(8,128)(2,1)S(1)} %shard_map.52.refs_0_, f32[128,2176]{1,0:T(8,128)S(1)} %get-tuple-element.12.refs_1_, f32[128,2176]{1,0:T(8,128)S(1)} %collective-permute-done.5.refs_2_, bf16[64,2176]{1,0:T(8,128)(2,1)S(1)} %collective-permute-done.6.refs_3_, ...), custom_call_target="tpu_custom_call" | custom-call | flops 8519680 | bytes 5963776 | tf_op jit(solution)/shard_map/pallas_call | solution.py:197
  (34 shorter events, 0.7 us)
Async XLA Ops:
  0.6 12.6 %collective-permute-start.1 = (bf16[64,2048]{1,0:T(8,128)(2,1)}, bf16[64,2048]{1,0:T(8,128)(2,1)S(1)}, u32[]{:S(2)}, u32[]{:S(2)}) collective-permute-start(bf16[64,2048]{1,0:T(8,128)(2,1)} %refs_1_.1), channel_id=1, source_target_pairs={{0,3},{1,2},{2,1},{3,0},{4,7},{5,6},{6,5},{7,4},{8,11},{9,10},{10,... | collective-permute-start | bytes 786440 | tf_op jit(solution)/shard_map/ppermute | solution.py:75
  5.8 27.3 %collective-permute-start = (bf16[64,2048]{1,0:T(8,128)(2,1)}, bf16[64,2048]{1,0:T(8,128)(2,1)S(1)}, u32[]{:S(2)}, u32[]{:S(2)}) collective-permute-start(bf16[64,2048]{1,0:T(8,128)(2,1)} %refs_1_.1), channel_id=1, source_target_pairs={{0,1},{1,0},{2,3},{3,2},{4,5},{5,4},{6,7},{7,6},{8,9},{9,8},{10,11... | collective-permute-start | bytes 786440 | tf_op jit(solution)/shard_map/ppermute | solution.py:75
  13.2 19.9 %collective-permute-start.2 = (bf16[64,2048]{1,0:T(8,128)(2,1)S(1)}, bf16[64,2048]{1,0:T(8,128)(2,1)S(1)}, u32[]{:S(2)}, u32[]{:S(2)}) collective-permute-start(bf16[64,2048]{1,0:T(8,128)(2,1)S(1)} %collective-permute-done.1.refs_3_), channel_id=1, source_target_pairs={{0,1},{1,0},{2,3},{3,2},{4,5},{5,4},{6,7},{7,6},{8,9},{9,8},{10,11... | collective-permute-start | bytes 786440 | tf_op jit(solution)/shard_map/ppermute | solution.py:75
  21.9 3.6 %copy-start.2 = (bf16[2176,2048]{1,0:T(8,128)(2,1)}, bf16[2176,2048]{1,0:T(8,128)(2,1)S(1)}, u32[]{:S(2)}) copy-start(bf16[2176,2048]{1,0:T(8,128)(2,1)S(1)} %shard_map.50.refs_5_) | copy-start | bytes 26738692
  25.4 7.6 %copy-start.4 = (bf16[64,2048]{1,0:T(8,128)(2,1)S(1)}, bf16[64,2048]{1,0:T(8,128)(2,1)}, u32[]{:S(2)}) copy-start(bf16[64,2048]{1,0:T(8,128)(2,1)} %refs_1_.1) | copy-start | bytes 786436
  29.6 3.5 %copy-start = (bf16[2176,2048]{1,0:T(8,128)(2,1)}, bf16[2176,2048]{1,0:T(8,128)(2,1)S(1)}, u32[]{:S(2)}) copy-start(bf16[2176,2048]{1,0:T(8,128)(2,1)S(1)} %shard_map.53.refs_1_) | copy-start | bytes 26738692
  33.1 3.5 %copy-start.3 = (bf16[2176,2048]{1,0:T(8,128)(2,1)S(1)}, bf16[2176,2048]{1,0:T(8,128)(2,1)}, u32[]{:S(2)}) copy-start(bf16[2176,2048]{1,0:T(8,128)(2,1)} %copy-done.2) | copy-start | bytes 26738692
  36.6 4.9 %copy-start.1 = (bf16[2176,2048]{1,0:T(8,128)(2,1)S(1)}, bf16[2176,2048]{1,0:T(8,128)(2,1)}, u32[]{:S(2)}) copy-start(bf16[2176,2048]{1,0:T(8,128)(2,1)} %copy-done) | copy-start | bytes 26738692
  39.8 16.1 %collective-permute-start.3 = (f32[128,2176]{1,0:T(8,128)S(1)}, f32[128,2176]{1,0:T(8,128)S(1)}, u32[]{:S(2)}, u32[]{:S(2)}) collective-permute-start(f32[128,2176]{1,0:T(8,128)S(1)} %get-tuple-element.10), channel_id=1, source_target_pairs={{0,4},{4,0},{8,12},{12,8},{1,5},{5,1},{9,13},{13,9},{2,6},{6,2},{1... | collective-permute-start | bytes 3342344 | tf_op jit(solution)/shard_map/ppermute | solution.py:75
  40.0 14.4 %collective-permute-start.16 = (bf16[128,2048]{1,0:T(8,128)(2,1)S(1)}, bf16[128,2048]{1,0:T(8,128)(2,1)S(1)}, u32[]{:S(2)}, u32[]{:S(2)}) collective-permute-start(bf16[128,2048]{1,0:T(8,128)(2,1)S(1)} %pad_maximum_fusion), channel_id=1, source_target_pairs={{0,16},{16,0},{1,17},{17,1},{2,18},{18,2},{3,19},{19,3},{4,20},{20... | collective-permute-start | bytes 1572872 | tf_op jit(solution)/shard_map/ppermute | solution.py:75
  41.6 2.9 %copy-start.5 = (bf16[64,6656]{1,0:T(8,128)(2,1)S(1)}, bf16[64,6656]{1,0:T(8,128)(2,1)}, u32[]{:S(2)}) copy-start(bf16[64,6656]{1,0:T(8,128)(2,1)} %param.4) | copy-start | bytes 2555908
  44.2 23.0 %collective-permute-start.5 = (f32[128,2176]{1,0:T(8,128)S(1)}, f32[128,2176]{1,0:T(8,128)S(1)}, u32[]{:S(2)}, u32[]{:S(2)}) collective-permute-start(f32[128,2176]{1,0:T(8,128)S(1)} %get-tuple-element.13), channel_id=1, source_target_pairs={{0,4},{4,0},{8,12},{12,8},{1,5},{5,1},{9,13},{13,9},{2,6},{6,2},{1... | collective-permute-start | bytes 3342344 | tf_op jit(solution)/shard_map/ppermute | solution.py:75
  44.5 24.3 %collective-permute-start.9 = (bf16[64,3328]{1,0:T(8,128)(2,1)S(1)}, bf16[64,3328]{1,0:T(8,128)(2,1)S(1)}, u32[]{:S(2)}, u32[]{:S(2)}) collective-permute-start(bf16[64,3328]{1,0:T(8,128)(2,1)S(1)} %get-tuple-element.17.refs_0_), channel_id=1, source_target_pairs={{0,8},{4,12},{8,0},{12,4},{1,9},{5,13},{9,1},{13,5},{2,10},{6,14},... | collective-permute-start | bytes 1277960 | tf_op jit(solution)/shard_map/ppermute | solution.py:75
  46.1 22.9 %collective-permute-start.10 = (bf16[64,3328]{1,0:T(8,128)(2,1)S(1)}, bf16[64,3328]{1,0:T(8,128)(2,1)S(1)}, u32[]{:S(2)}, u32[]{:S(2)}) collective-permute-start(bf16[64,3328]{1,0:T(8,128)(2,1)S(1)} %get-tuple-element.17.refs_0_), channel_id=1, source_target_pairs={{0,4},{4,0},{8,12},{12,8},{1,5},{5,1},{9,13},{13,9},{2,6},{6,2},{1... | collective-permute-start | bytes 1277960 | tf_op jit(solution)/shard_map/ppermute | solution.py:75
  54.4 11.4 %collective-permute-start.12 = (bf16[64,3328]{1,0:T(8,128)(2,1)S(1)}, bf16[64,3328]{1,0:T(8,128)(2,1)S(1)}, u32[]{:S(2)}, u32[]{:S(2)}) collective-permute-start(bf16[64,3328]{1,0:T(8,128)(2,1)S(1)} %get-tuple-element.16), channel_id=1, source_target_pairs={{0,16},{16,0},{1,17},{17,1},{2,18},{18,2},{3,19},{19,3},{4,20},{20... | collective-permute-start | bytes 1277960 | tf_op jit(solution)/shard_map/ppermute | solution.py:75
  55.9 21.6 %collective-permute-start.7 = (f32[128,2304]{1,0:T(8,128)S(1)}, f32[128,2304]{1,0:T(8,128)S(1)}, u32[]{:S(2)}, u32[]{:S(2)}) collective-permute-start(f32[128,2304]{1,0:T(8,128)S(1)} %get-tuple-element.15), channel_id=1, source_target_pairs={{0,4},{4,0},{8,12},{12,8},{1,5},{5,1},{9,13},{13,9},{2,6},{6,2},{1... | collective-permute-start | bytes 3538952 | tf_op jit(solution)/shard_map/ppermute | solution.py:75
  65.7 11.9 %collective-permute-start.17 = (bf16[64,2048]{1,0:T(8,128)(2,1)S(1)}, bf16[64,2048]{1,0:T(8,128)(2,1)S(1)}, u32[]{:S(2)}, u32[]{:S(2)}) collective-permute-start(bf16[64,2048]{1,0:T(8,128)(2,1)S(1)} %collective-permute-done.refs_2_), channel_id=1, source_target_pairs={{0,16},{16,0},{1,17},{17,1},{2,18},{18,2},{3,19},{19,3},{4,20},{20... | collective-permute-start | bytes 786440 | tf_op jit(solution)/shard_map/ppermute | solution.py:75
  67.2 10.2 %collective-permute-start.13 = (bf16[64,3328]{1,0:T(8,128)(2,1)S(1)}, bf16[64,3328]{1,0:T(8,128)(2,1)S(1)}, u32[]{:S(2)}, u32[]{:S(2)}) collective-permute-start(bf16[64,3328]{1,0:T(8,128)(2,1)S(1)} %collective-permute-done.12.refs_4_), channel_id=1, source_target_pairs={{0,8},{4,12},{8,0},{12,4},{1,9},{5,13},{9,1},{13,5},{2,10},{6,14},... | collective-permute-start | bytes 1277960 | tf_op jit(solution)/shard_map/ppermute | solution.py:75
  68.9 10.8 %collective-permute-start.14 = (bf16[64,3328]{1,0:T(8,128)(2,1)S(1)}, bf16[64,3328]{1,0:T(8,128)(2,1)S(1)}, u32[]{:S(2)}, u32[]{:S(2)}) collective-permute-start(bf16[64,3328]{1,0:T(8,128)(2,1)S(1)} %collective-permute-done.12.refs_4_), channel_id=1, source_target_pairs={{0,4},{4,0},{8,12},{12,8},{1,5},{5,1},{9,13},{13,9},{2,6},{6,2},{1... | collective-permute-start | bytes 1277960 | tf_op jit(solution)/shard_map/ppermute | solution.py:75
  69.0 10.2 %collective-permute-start.11 = (bf16[64,3328]{1,0:T(8,128)(2,1)S(1)}, bf16[64,3328]{1,0:T(8,128)(2,1)S(1)}, u32[]{:S(2)}, u32[]{:S(2)}) collective-permute-start(bf16[64,3328]{1,0:T(8,128)(2,1)S(1)} %collective-permute-done.9.refs_1_), channel_id=1, source_target_pairs={{0,4},{4,0},{8,12},{12,8},{1,5},{5,1},{9,13},{13,9},{2,6},{6,2},{1... | collective-permute-start | bytes 1277960 | tf_op jit(solution)/shard_map/ppermute | solution.py:75
  77.5 6.4 %collective-permute-start.18 = (bf16[64,2048]{1,0:T(8,128)(2,1)S(1)}, bf16[64,2048]{1,0:T(8,128)(2,1)S(1)}, u32[]{:S(2)}, u32[]{:S(2)}) collective-permute-start(bf16[64,2048]{1,0:T(8,128)(2,1)S(1)} %slice.31), channel_id=1, source_target_pairs={{0,1},{1,0},{2,3},{3,2},{4,5},{5,4},{6,7},{7,6},{8,9},{9,8},{10,11... | collective-permute-start | bytes 786440 | tf_op jit(solution)/shard_map/ppermute | solution.py:75
  77.5 6.4 %collective-permute-start.15 = (bf16[64,3328]{1,0:T(8,128)(2,1)S(1)}, bf16[64,3328]{1,0:T(8,128)(2,1)S(1)}, u32[]{:S(2)}, u32[]{:S(2)}) collective-permute-start(bf16[64,3328]{1,0:T(8,128)(2,1)S(1)} %collective-permute-done.13.refs_5_), channel_id=1, source_target_pairs={{0,4},{4,0},{8,12},{12,8},{1,5},{5,1},{9,13},{13,9},{2,6},{6,2},{1... | collective-permute-start | bytes 1277960 | tf_op jit(solution)/shard_map/ppermute | solution.py:75
  77.7 16.2 %collective-permute-start.4 = (bf16[64,2176]{1,0:T(8,128)(2,1)S(1)}, bf16[64,2176]{1,0:T(8,128)(2,1)S(1)}, u32[]{:S(2)}, u32[]{:S(2)}) collective-permute-start(bf16[64,2176]{1,0:T(8,128)(2,1)S(1)} %fusion.2), channel_id=1, source_target_pairs={{0,8},{4,12},{8,0},{12,4},{1,9},{5,13},{9,1},{13,5},{2,10},{6,14},... | collective-permute-start | bytes 835592 | tf_op jit(solution)/shard_map/ppermute | solution.py:75
  79.2 15.0 %collective-permute-start.6 = (bf16[64,2176]{1,0:T(8,128)(2,1)S(1)}, bf16[64,2176]{1,0:T(8,128)(2,1)S(1)}, u32[]{:S(2)}, u32[]{:S(2)}) collective-permute-start(bf16[64,2176]{1,0:T(8,128)(2,1)S(1)} %fusion.3), channel_id=1, source_target_pairs={{0,8},{4,12},{8,0},{12,4},{1,9},{5,13},{9,1},{13,5},{2,10},{6,14},... | collective-permute-start | bytes 835592 | tf_op jit(solution)/shard_map/ppermute | solution.py:75
  79.8 19.3 %collective-permute-start.8 = (bf16[64,2304]{1,0:T(8,128)(2,1)S(1)}, bf16[64,2304]{1,0:T(8,128)(2,1)S(1)}, u32[]{:S(2)}, u32[]{:S(2)}) collective-permute-start(bf16[64,2304]{1,0:T(8,128)(2,1)S(1)} %fusion), channel_id=1, source_target_pairs={{0,8},{4,12},{8,0},{12,4},{1,9},{5,13},{9,1},{13,5},{2,10},{6,14},... | collective-permute-start | bytes 884744 | tf_op jit(solution)/shard_map/ppermute | solution.py:75
where the time goes:
time: 101 us
  waiting for transfers between devices  33.7 us (33%)
  Pallas kernels  32.8 us (32%)
  starting transfers between devices  21.8 us (22%)
  local copies, waits for them, and re-layouts  10.6 us (10%)
    ppermute x19, waiting for transfers between devices, swap(): return lax.ppermute(x, axis, [(i, i ^ mask) for i in range(n)])  33.7 us
    ppermute x19, starting transfers between devices, swap(): return lax.ppermute(x, axis, [(i, i ^ mask) for i in range(n)])  21.8 us
    pallas_call x3, Pallas kernels, load(): pl.pallas_call(functools.partial(load_kernel, spans), in_specs=[pl.BlockS...  12.7 us
    unnamed x12, local copies, waits for them, and re-layouts  10.6 us
    pallas_call x1, Pallas kernels, weight_product(): pl.pallas_call(functools.partial(weight_kernel, len(hidden), pieces), in_...  10 us
    pallas_call x3, Pallas kernels, product(): pl.pallas_call(functools.partial(product_kernel, len(blocks), spans), in_...  8.49 us
  transfers between devices with their start and end apart: 19, of which 6 were waited for; matrix products, arithmetic and copies ran while one was open for 1% of the time, Pallas kernels for 28%

commit v1 on v0

--- a/solution.py
+++ b/solution.py
@@ -13,7 +13,7 @@
 EARLY = 1
 STEPS = (8, 8, 6, 4)
 ACROSS = 1
-SHARES = (17, 17, 18)
+SHARES = (12, 13, 13, 14)
 CHUNKS = len(SHARES)
 NT = (((1,), (1,)), ((), ()))
 TN = (((0,), (0,)), ((), ()))
@@ -236,7 +236,7 @@
     out, held, slots, sem = refs[-4:]
     half = own.shape[0]
     held[:half, :] = own[...]
-    for peer, places in zip(peers, ((0, 2), (1,), (3,))):
+    for peer, places in zip(peers, ((0, 2, 1), (3,))):
         for i, place in enumerate(places):
             start = pl.multiple_of(half + at[place] * rows, rows)
             held[pl.ds(start, rows), :] = peer[i * rows : (i + 1) * rows]
@@ -292,11 +292,9 @@
     pair = swap(grad_out, "col", 1)
     rev = swap(grad_out, "col", 3)
     s2 = swap(rev, "col", 1)
-    two = jnp.concatenate([grad_out, rev])
-    y_two = swap(two, "dp", 1)
-    y_pair = swap(pair, "dp", 1)
-    y_rev = y_two[grad_out.shape[0] :]
-    y_s2 = swap(y_rev, "col", 1)
+    three = jnp.concatenate([grad_out, rev, pair])
+    y_three = swap(three, "dp", 1)
+    y_s2 = swap(s2, "dp", 1)
     h_give = lax.dynamic_slice_in_dim(saved_hidden, (1 - d) * half, half, 1)
     h_mine = lax.dynamic_slice_in_dim(saved_hidden, d * half, half, 1)
     h_peer = swap(h_give, "dp", 1)
@@ -329,7 +327,7 @@
         at,
         [mine[0], mine[2], mate[0], mate[2], mine[1], mine[3], mate[1], mate[3]],
         grads,
-        [y_two, y_pair, y_s2],
+        [y_three, y_s2],
     )
     return input_grad, weight_grad
 

time: 101 us -> 99 us (0.980)
  local copies, waits for them, and re-layouts: 10.6 us -> 7.18 us
  waiting for transfers between devices: 33.7 us -> 36.7 us
  starting transfers between devices: 21.8 us -> 19.9 us
    unnamed x12 -> x14, local copies, waits for them, and re-layouts: 10.6 us -> 7.11 us
    ppermute x19 -> x20, waiting for transfers between devices: 33.7 us -> 36.7 us  [swap(): return lax.ppermute(x, axis, [(i, i ^ mask) for i in range(n)])]
    ppermute x19 -> x20, starting transfers between devices: 21.8 us -> 19.9 us  [swap(): return lax.ppermute(x, axis, [(i, i ^ mask) for i in range(n)])]
    pallas_call x3 -> x4, Pallas kernels: 8.49 us -> 8.65 us  [product(): pl.pallas_call(functools.partial(product_kernel, len(blocks), spans), in_...]
  transfers between devices with their start and end apart: 19 -> 20, of which waited for: 6 -> 6; matrix products, arithmetic and copies ran while one was open for 1% -> 1% of each run, Pallas kernels for 28% -> 30%
where the time goes in v1:
time: 99 us; the launch traced here: 98.9 us
  waiting for transfers between devices  36.7 us (37%)
  Pallas kernels  33.4 us (34%)
  starting transfers between devices  19.9 us (20%)
  local copies, waits for them, and re-layouts  7.18 us (7%)
  between operations  1.02 us (1%)
    ppermute x20, waiting for transfers between devices, swap(): return lax.ppermute(x, axis, [(i, i ^ mask) for i in range(n)])  36.7 us
    ppermute x20, starting transfers between devices, swap(): return lax.ppermute(x, axis, [(i, i ^ mask) for i in range(n)])  19.9 us
    pallas_call x3, Pallas kernels, load(): pl.pallas_call(functools.partial(load_kernel, spans), in_specs=[pl.BlockS...  13.1 us
    pallas_call x1, Pallas kernels, weight_product(): pl.pallas_call(functools.partial(weight_kernel, len(hidden), pieces), in_...  10 us
    pallas_call x4, Pallas kernels, product(): pl.pallas_call(functools.partial(product_kernel, len(blocks), spans), in_...  8.65 us
    unnamed x14, local copies, waits for them, and re-layouts  7.11 us
  transfers between devices with their start and end apart: 20, of which 6 were waited for; matrix products, arithmetic and copies ran while one was open for 1% of the time, Pallas kernels for 30%

profile of v1, /device:TPU:0, one launch (start us, length us, event | category | flops | bytes accessed | tf_op | source)
XLA Modules:
  0.0 98.9 jit_solution(9016373434779960325)
XLA Ops:
  0.6 5.1 %collective-permute-start.1 = (bf16[64,2048]{1,0:T(8,128)(2,1)}, bf16[64,2048]{1,0:T(8,128)(2,1)S(1)}, u32[]{:S(2)}, u32[]{:S(2)}) collective-permute-start(bf16[64,2048]{1,0:T(8,128)(2,1)} %refs_1_.1), channel_id=1, source_target_pairs={{0,3},{1,2},{2,1},{3,0},{4,7},{5,6},{6,5},{7,4},{8,11},{9,10},{10,... | collective-permute-start | bytes 786440 | tf_op jit(solution)/shard_map/ppermute | solution.py:75
  5.8 7.5 %collective-permute-done.1.refs_3_ = bf16[64,2048]{1,0:T(8,128)(2,1)S(1)} collective-permute-done((bf16[64,2048]{1,0:T(8,128)(2,1)}, bf16[64,2048]{1,0:T(8,128)(2,1)S(1)}, u32[]{:S(2)}, u32[]{:S(2)}) %collective-permute-start.1) | collective-permute-done | bytes 262176 | tf_op jit(solution)/shard_map/ppermute | solution.py:75
  13.2 4.4 %collective-permute-start.2 = (bf16[64,2048]{1,0:T(8,128)(2,1)S(1)}, bf16[64,2048]{1,0:T(8,128)(2,1)S(1)}, u32[]{:S(2)}, u32[]{:S(2)}) collective-permute-start(bf16[64,2048]{1,0:T(8,128)(2,1)S(1)} %collective-permute-done.1.refs_3_), channel_id=1, source_target_pairs={{0,1},{1,0},{2,3},{3,2},{4,5},{5,4},{6,7},{7,6},{8,9},{9,8},{10,11... | collective-permute-start | bytes 786440 | tf_op jit(solution)/shard_map/ppermute | solution.py:75
  17.7 4.2 %shard_map.50.refs_5_.refs_1_ = bf16[2176,2048]{1,0:T(8,128)(2,1)S(1)} custom-call(s32[4]{0:T(128)S(1)} %pad_add_fusion.at.refs_0_, bf16[6656,2048]{1,0:T(8,128)(2,1)} %w.5), custom_call_target="tpu_custom_call" | custom-call | bytes 8912896 | tf_op jit(solution)/shard_map/pallas_call | solution.py:104
  21.9 3.6 %copy-done = bf16[2176,2048]{1,0:T(8,128)(2,1)} copy-done((bf16[2176,2048]{1,0:T(8,128)(2,1)}, bf16[2176,2048]{1,0:T(8,128)(2,1)S(1)}, u32[]{:S(2)}) %copy-start) | copy-done | bytes 8912920
  25.5 3.5 %copy-done.1 = bf16[2176,2048]{1,0:T(8,128)(2,1)S(1)} copy-done((bf16[2176,2048]{1,0:T(8,128)(2,1)S(1)}, bf16[2176,2048]{1,0:T(8,128)(2,1)}, u32[]{:S(2)}) %copy-start.1) | copy-done | bytes 8912920
  29.0 2.4 %shard_map.51 = (f32[128,1536]{1,0:T(8,128)S(1)}, f32[128,1536]{1,0:T(8,128)S(1)}, bf16[256,2048]{1,0:T(8,128)(2,1)S(1)}) custom-call(s32[4]{0:T(128)S(1)} %pad_add_fusion.at.refs_0_, bf16[64,2048]{1,0:T(8,128)(2,1)S(1)} %copy-done.2, bf16[64,2048]{1,0:T(8,128)(2,1)S(1)} %collective-permute-done.refs_2_, ...), custom_call_target="tpu_custom_call" | custom-call | flops 1610612736 | bytes 6291456 | tf_op jit(solution)/shard_map/pallas_call | solution.py:146
  31.5 1.6 %collective-permute-start.11 = (bf16[64,3328]{1,0:T(8,128)(2,1)S(1)}, bf16[64,3328]{1,0:T(8,128)(2,1)S(1)}, u32[]{:S(2)}, u32[]{:S(2)}) collective-permute-start(bf16[64,3328]{1,0:T(8,128)(2,1)S(1)} %get-tuple-element.21.refs_0_), channel_id=1, source_target_pairs={{0,8},{4,12},{8,0},{12,4},{1,9},{5,13},{9,1},{13,5},{2,10},{6,14},... | collective-permute-start | bytes 1277960 | tf_op jit(solution)/shard_map/ppermute | solution.py:75
  33.1 0.2 collective-permute-start.12
  33.3 1.5 %collective-permute-start.14 = (bf16[64,3328]{1,0:T(8,128)(2,1)S(1)}, bf16[64,3328]{1,0:T(8,128)(2,1)S(1)}, u32[]{:S(2)}, u32[]{:S(2)}) collective-permute-start(bf16[64,3328]{1,0:T(8,128)(2,1)S(1)} %get-tuple-element.20), channel_id=1, source_target_pairs={{0,16},{16,0},{1,17},{17,1},{2,18},{18,2},{3,19},{19,3},{4,20},{20... | collective-permute-start | bytes 1277960 | tf_op jit(solution)/shard_map/ppermute | solution.py:75
  34.8 4.4 %shard_map.53.refs_2_.refs_1_ = bf16[2176,2048]{1,0:T(8,128)(2,1)S(1)} custom-call(s32[4]{0:T(128)S(1)} %pad_add_fusion.at.refs_0_, bf16[6656,2048]{1,0:T(8,128)(2,1)} %w.5), custom_call_target="tpu_custom_call" | custom-call | bytes 8912896 | tf_op jit(solution)/shard_map/pallas_call | solution.py:104
  39.3 4.5 %shard_map.55.refs_2_.refs_1_ = bf16[2304,2048]{1,0:T(8,128)(2,1)S(1)} custom-call(s32[4]{0:T(128)S(1)} %pad_add_fusion.at.refs_0_, bf16[6656,2048]{1,0:T(8,128)(2,1)} %w.5), custom_call_target="tpu_custom_call" | custom-call | bytes 9437184 | tf_op jit(solution)/shard_map/pallas_call | solution.py:104
  43.9 2.1 %shard_map.54 = (f32[128,1664]{1,0:T(8,128)S(1)}, f32[128,1664]{1,0:T(8,128)S(1)}) custom-call(bf16[256,2048]{1,0:T(8,128)(2,1)S(1)} %get-tuple-element.13.refs_0_.refs_8_, bf16[2176,2048]{1,0:T(8,128)(2,1)S(1)} %bitcast.5, bf16[2176,2048]{1,0:T(8,128)(2,1)S(1)} %shard_map.53.refs_2_.refs_1_), custom_call_target="tpu_custom_call" | custom-call | flops 1744830464 | bytes 6815744 | tf_op jit(solution)/shard_map/pallas_call | solution.py:146
  46.1 2.1 %shard_map.56 = (f32[128,1664]{1,0:T(8,128)S(1)}, f32[128,1664]{1,0:T(8,128)S(1)}) custom-call(bf16[256,2048]{1,0:T(8,128)(2,1)S(1)} %get-tuple-element.13.refs_0_.refs_8_, bf16[2176,2048]{1,0:T(8,128)(2,1)S(1)} %shard_map.53.refs_2_.refs_1_, bf16[2304,2048]{1,0:T(8,128)(2,1)S(1)} %shard_map.55.refs_2_.refs_1_), custom_call_target="tpu_custom_call" | custom-call | flops 1744830464 | bytes 6815744 | tf_op jit(solution)/shard_map/pallas_call | solution.py:146
  48.2 2.1 %shard_map.57 = (f32[128,1792]{1,0:T(8,128)S(1)}, f32[128,1792]{1,0:T(8,128)S(1)}) custom-call(bf16[256,2048]{1,0:T(8,128)(2,1)S(1)} %get-tuple-element.13.refs_0_.refs_8_, bf16[2304,2048]{1,0:T(8,128)(2,1)S(1)} %shard_map.55.refs_2_.refs_1_), custom_call_target="tpu_custom_call" | custom-call | flops 1879048192 | bytes 7340032 | tf_op jit(solution)/shard_map/pallas_call | solution.py:146
  50.3 0.5 collective-permute-start.7
  51.2 0.6 collective-permute-start.18
  51.8 1.1 %collective-permute-done.7.refs_5_ = f32[128,1664]{1,0:T(8,128)S(1)} collective-permute-done((f32[128,1664]{1,0:T(8,128)S(1)}, f32[128,1664]{1,0:T(8,128)S(1)}, u32[]{:S(2)}, u32[]{:S(2)}) %collective-permute-start.7) | collective-permute-done | bytes 852000 | tf_op jit(solution)/shard_map/ppermute | solution.py:75
  52.9 0.5 collective-permute-start.15
  53.7 0.4 collective-permute-start.13
  54.1 10.8 %collective-permute-done.15.refs_5_ = bf16[64,3328]{1,0:T(8,128)(2,1)S(1)} collective-permute-done((bf16[64,3328]{1,0:T(8,128)(2,1)S(1)}, bf16[64,3328]{1,0:T(8,128)(2,1)S(1)}, u32[]{:S(2)}, u32[]{:S(2)}) %collective-permute-start.15) | collective-permute-done | bytes 426016 | tf_op jit(solution)/shard_map/ppermute | solution.py:75
  65.0 0.5 collective-permute-start.19
  65.6 11.2 %collective-permute-done.19.refs_10_ = bf16[64,2048]{1,0:T(8,128)(2,1)S(1)} collective-permute-done((bf16[64,2048]{1,0:T(8,128)(2,1)S(1)}, bf16[64,2048]{1,0:T(8,128)(2,1)S(1)}, u32[]{:S(2)}, u32[]{:S(2)}) %collective-permute-start.19) | collective-permute-done | bytes 262176 | tf_op jit(solution)/shard_map/ppermute | solution.py:75
  76.9 0.5 collective-permute-start.4
  77.4 1.5 %collective-permute-start.6 = (bf16[64,1664]{1,0:T(8,128)(2,1)S(1)}, bf16[64,1664]{1,0:T(8,128)(2,1)S(1)}, u32[]{:S(2)}, u32[]{:S(2)}) collective-permute-start(bf16[64,1664]{1,0:T(8,128)(2,1)S(1)} %fusion.2), channel_id=1, source_target_pairs={{0,8},{4,12},{8,0},{12,4},{1,9},{5,13},{9,1},{13,5},{2,10},{6,14},... | collective-permute-start | bytes 638984 | tf_op jit(solution)/shard_map/ppermute | solution.py:75
  78.9 0.5 collective-permute-start.8
  79.4 1.5 %collective-permute-start.10 = (bf16[64,1792]{1,0:T(8,128)(2,1)S(1)}, bf16[64,1792]{1,0:T(8,128)(2,1)S(1)}, u32[]{:S(2)}, u32[]{:S(2)}) collective-permute-start(bf16[64,1792]{1,0:T(8,128)(2,1)S(1)} %fusion), channel_id=1, source_target_pairs={{0,8},{4,12},{8,0},{12,4},{1,9},{5,13},{9,1},{13,5},{2,10},{6,14},... | collective-permute-start | bytes 688136 | tf_op jit(solution)/shard_map/ppermute | solution.py:75
  80.9 10.0 %shard_map.59 = bf16[3328,2048]{1,0:T(8,128)(2,1)} custom-call(s32[4]{0:T(128)S(1)} %pad_add_fusion.at.refs_0_, bf16[64,3328]{1,0:T(8,128)(2,1)S(1)} %get-tuple-element.21.refs_0_, bf16[64,3328]{1,0:T(8,128)(2,1)S(1)} %collective-permute-done.11.refs_1_, bf16[64,3328]{1,0:T(8,128)(2,1)S(1)} %collective-permute-done.12.refs_2_, ...), custom_call_target="tpu_custom_call" | custom-call | flops 6979321856 | bytes 13631488 | tf_op jit(solution)/shard_map/pallas_call | solution.py:268
  91.0 0.2 shard_map.52.refs_0_
  91.2 2.5 %collective-permute-done.8.refs_6_ = bf16[64,1664]{1,0:T(8,128)(2,1)S(1)} collective-permute-done((bf16[64,1664]{1,0:T(8,128)(2,1)S(1)}, bf16[64,1664]{1,0:T(8,128)(2,1)S(1)}, u32[]{:S(2)}, u32[]{:S(2)}) %collective-permute-start.8) | collective-permute-done | bytes 213024 | tf_op jit(solution)/shard_map/ppermute | solution.py:75
  93.8 3.6 %collective-permute-done.10.refs_9_ = bf16[64,1792]{1,0:T(8,128)(2,1)S(1)} collective-permute-done((bf16[64,1792]{1,0:T(8,128)(2,1)S(1)}, bf16[64,1792]{1,0:T(8,128)(2,1)S(1)}, u32[]{:S(2)}, u32[]{:S(2)}) %collective-permute-start.10) | collective-permute-done | bytes 229408 | tf_op jit(solution)/shard_map/ppermute | solution.py:75
  97.3 1.4 %shard_map.58 = bf16[64,6656]{1,0:T(8,128)(2,1)} custom-call(bf16[64,1536]{1,0:T(8,128)(2,1)S(1)} %shard_map.52.refs_0_, f32[128,1664]{1,0:T(8,128)S(1)} %get-tuple-element.14.refs_1_, f32[128,1664]{1,0:T(8,128)S(1)} %collective-permute-done.5.refs_2_, bf16[64,1664]{1,0:T(8,128)(2,1)S(1)} %collective-permute-done.6.refs_3_, ...), custom_call_target="tpu_custom_call" | custom-call | flops 8519680 | bytes 5963776 | tf_op jit(solution)/shard_map/pallas_call | solution.py:197
  (40 shorter events, 1.2 us)
Async XLA Ops:
  0.6 12.6 %collective-permute-start.1 = (bf16[64,2048]{1,0:T(8,128)(2,1)}, bf16[64,2048]{1,0:T(8,128)(2,1)S(1)}, u32[]{:S(2)}, u32[]{:S(2)}) collective-permute-start(bf16[64,2048]{1,0:T(8,128)(2,1)} %refs_1_.1), channel_id=1, source_target_pairs={{0,3},{1,2},{2,1},{3,0},{4,7},{5,6},{6,5},{7,4},{8,11},{9,10},{10,... | collective-permute-start | bytes 786440 | tf_op jit(solution)/shard_map/ppermute | solution.py:75
  5.8 19.7 %collective-permute-start = (bf16[64,2048]{1,0:T(8,128)(2,1)}, bf16[64,2048]{1,0:T(8,128)(2,1)S(1)}, u32[]{:S(2)}, u32[]{:S(2)}) collective-permute-start(bf16[64,2048]{1,0:T(8,128)(2,1)} %refs_1_.1), channel_id=1, source_target_pairs={{0,1},{1,0},{2,3},{3,2},{4,5},{5,4},{6,7},{7,6},{8,9},{9,8},{10,11... | collective-permute-start | bytes 786440 | tf_op jit(solution)/shard_map/ppermute | solution.py:75
  13.2 12.2 %collective-permute-start.2 = (bf16[64,2048]{1,0:T(8,128)(2,1)S(1)}, bf16[64,2048]{1,0:T(8,128)(2,1)S(1)}, u32[]{:S(2)}, u32[]{:S(2)}) collective-permute-start(bf16[64,2048]{1,0:T(8,128)(2,1)S(1)} %collective-permute-done.1.refs_3_), channel_id=1, source_target_pairs={{0,1},{1,0},{2,3},{3,2},{4,5},{5,4},{6,7},{7,6},{8,9},{9,8},{10,11... | collective-permute-start | bytes 786440 | tf_op jit(solution)/shard_map/ppermute | solution.py:75
  17.7 7.8 %copy-start.2 = (bf16[64,2048]{1,0:T(8,128)(2,1)S(1)}, bf16[64,2048]{1,0:T(8,128)(2,1)}, u32[]{:S(2)}) copy-start(bf16[64,2048]{1,0:T(8,128)(2,1)} %refs_1_.1) | copy-start | bytes 786436
  17.7 13.8 %copy-start.3 = (bf16[64,6656]{1,0:T(8,128)(2,1)S(1)}, bf16[64,6656]{1,0:T(8,128)(2,1)}, u32[]{:S(2)}) copy-start(bf16[64,6656]{1,0:T(8,128)(2,1)} %param.4) | copy-start | bytes 2555908
  21.9 3.6 %copy-start = (bf16[2176,2048]{1,0:T(8,128)(2,1)}, bf16[2176,2048]{1,0:T(8,128)(2,1)S(1)}, u32[]{:S(2)}) copy-start(bf16[2176,2048]{1,0:T(8,128)(2,1)S(1)} %shard_map.50.refs_5_.refs_1_) | copy-start | bytes 26738692
  25.5 3.5 %copy-start.1 = (bf16[2176,2048]{1,0:T(8,128)(2,1)S(1)}, bf16[2176,2048]{1,0:T(8,128)(2,1)}, u32[]{:S(2)}) copy-start(bf16[2176,2048]{1,0:T(8,128)(2,1)} %copy-done) | copy-start | bytes 26738692
  31.4 18.9 %collective-permute-start.3 = (f32[128,1536]{1,0:T(8,128)S(1)}, f32[128,1536]{1,0:T(8,128)S(1)}, u32[]{:S(2)}, u32[]{:S(2)}) collective-permute-start(f32[128,1536]{1,0:T(8,128)S(1)} %get-tuple-element.12), channel_id=1, source_target_pairs={{0,4},{4,0},{8,12},{12,8},{1,5},{5,1},{9,13},{13,9},{2,6},{6,2},{1... | collective-permute-start | bytes 2359304 | tf_op jit(solution)/shard_map/ppermute | solution.py:75
  31.5 22.0 %collective-permute-start.11 = (bf16[64,3328]{1,0:T(8,128)(2,1)S(1)}, bf16[64,3328]{1,0:T(8,128)(2,1)S(1)}, u32[]{:S(2)}, u32[]{:S(2)}) collective-permute-start(bf16[64,3328]{1,0:T(8,128)(2,1)S(1)} %get-tuple-element.21.refs_0_), channel_id=1, source_target_pairs={{0,8},{4,12},{8,0},{12,4},{1,9},{5,13},{9,1},{13,5},{2,10},{6,14},... | collective-permute-start | bytes 1277960 | tf_op jit(solution)/shard_map/ppermute | solution.py:75
  33.1 20.6 %collective-permute-start.12 = (bf16[64,3328]{1,0:T(8,128)(2,1)S(1)}, bf16[64,3328]{1,0:T(8,128)(2,1)S(1)}, u32[]{:S(2)}, u32[]{:S(2)}) collective-permute-start(bf16[64,3328]{1,0:T(8,128)(2,1)S(1)} %get-tuple-element.21.refs_0_), channel_id=1, source_target_pairs={{0,4},{4,0},{8,12},{12,8},{1,5},{5,1},{9,13},{13,9},{2,6},{6,2},{1... | collective-permute-start | bytes 1277960 | tf_op jit(solution)/shard_map/ppermute | solution.py:75
  33.3 17.9 %collective-permute-start.14 = (bf16[64,3328]{1,0:T(8,128)(2,1)S(1)}, bf16[64,3328]{1,0:T(8,128)(2,1)S(1)}, u32[]{:S(2)}, u32[]{:S(2)}) collective-permute-start(bf16[64,3328]{1,0:T(8,128)(2,1)S(1)} %get-tuple-element.20), channel_id=1, source_target_pairs={{0,16},{16,0},{1,17},{17,1},{2,18},{18,2},{3,19},{19,3},{4,20},{20... | collective-permute-start | bytes 1277960 | tf_op jit(solution)/shard_map/ppermute | solution.py:75
  34.8 9.0 %slice-start = ((s8[8912896]{0:T(1024)(128)(4,1)}), s8[4194304]{0:T(1024)(128)(4,1)S(1)}, s32[]{:S(2)}) async-start(s8[8912896]{0:T(1024)(128)(4,1)} %bitcast.4), calls=%async_computation | async-start | bytes 8388608
  34.8 9.0 %slice-start.1 = ((s8[8912896]{0:T(1024)(128)(4,1)}), s8[4194304]{0:T(1024)(128)(4,1)S(1)}, s32[]{:S(2)}) async-start(s8[8912896]{0:T(1024)(128)(4,1)} %bitcast.4), calls=%async_computation.1 | async-start | bytes 8388608
  39.3 4.6 %slice-start.2 = ((s8[8912896]{0:T(1024)(128)(4,1)}), s8[524288]{0:T(1024)(128)(4,1)S(1)}, s32[]{:S(2)}) async-start(s8[8912896]{0:T(1024)(128)(4,1)} %bitcast.4), calls=%async_computation.2 | async-start | bytes 1048576
  46.0 5.0 %collective-permute-start.5 = (f32[128,1664]{1,0:T(8,128)S(1)}, f32[128,1664]{1,0:T(8,128)S(1)}, u32[]{:S(2)}, u32[]{:S(2)}) collective-permute-start(f32[128,1664]{1,0:T(8,128)S(1)} %get-tuple-element.15), channel_id=1, source_target_pairs={{0,4},{4,0},{8,12},{12,8},{1,5},{5,1},{9,13},{13,9},{2,6},{6,2},{1... | collective-permute-start | bytes 2555912 | tf_op jit(solution)/shard_map/ppermute | solution.py:75
  50.3 2.5 %collective-permute-start.7 = (f32[128,1664]{1,0:T(8,128)S(1)}, f32[128,1664]{1,0:T(8,128)S(1)}, u32[]{:S(2)}, u32[]{:S(2)}) collective-permute-start(f32[128,1664]{1,0:T(8,128)S(1)} %get-tuple-element.17), channel_id=1, source_target_pairs={{0,4},{4,0},{8,12},{12,8},{1,5},{5,1},{9,13},{13,9},{2,6},{6,2},{1... | collective-permute-start | bytes 2555912 | tf_op jit(solution)/shard_map/ppermute | solution.py:75
  51.0 14.5 %collective-permute-start.9 = (f32[128,1792]{1,0:T(8,128)S(1)}, f32[128,1792]{1,0:T(8,128)S(1)}, u32[]{:S(2)}, u32[]{:S(2)}) collective-permute-start(f32[128,1792]{1,0:T(8,128)S(1)} %get-tuple-element.19), channel_id=1, source_target_pairs={{0,4},{4,0},{8,12},{12,8},{1,5},{5,1},{9,13},{13,9},{2,6},{6,2},{1... | collective-permute-start | bytes 2752520 | tf_op jit(solution)/shard_map/ppermute | solution.py:75
  51.2 28.2 %collective-permute-start.18 = (bf16[192,2048]{1,0:T(8,128)(2,1)S(1)}, bf16[192,2048]{1,0:T(8,128)(2,1)S(1)}, u32[]{:S(2)}, u32[]{:S(2)}) collective-permute-start(bf16[192,2048]{1,0:T(8,128)(2,1)S(1)} %pad_maximum_fusion), channel_id=1, source_target_pairs={{0,16},{16,0},{1,17},{17,1},{2,18},{18,2},{3,19},{19,3},{4,20},{20... | collective-permute-start | bytes 2359304 | tf_op jit(solution)/shard_map/ppermute | solution.py:75
  52.9 12.1 %collective-permute-start.15 = (bf16[64,3328]{1,0:T(8,128)(2,1)S(1)}, bf16[64,3328]{1,0:T(8,128)(2,1)S(1)}, u32[]{:S(2)}, u32[]{:S(2)}) collective-permute-start(bf16[64,3328]{1,0:T(8,128)(2,1)S(1)} %collective-permute-done.14.refs_4_), channel_id=1, source_target_pairs={{0,8},{4,12},{8,0},{12,4},{1,9},{5,13},{9,1},{13,5},{2,10},{6,14},... | collective-permute-start | bytes 1277960 | tf_op jit(solution)/shard_map/ppermute | solution.py:75
  53.6 25.3 %collective-permute-start.16 = (bf16[64,3328]{1,0:T(8,128)(2,1)S(1)}, bf16[64,3328]{1,0:T(8,128)(2,1)S(1)}, u32[]{:S(2)}, u32[]{:S(2)}) collective-permute-start(bf16[64,3328]{1,0:T(8,128)(2,1)S(1)} %collective-permute-done.14.refs_4_), channel_id=1, source_target_pairs={{0,4},{4,0},{8,12},{12,8},{1,5},{5,1},{9,13},{13,9},{2,6},{6,2},{1... | collective-permute-start | bytes 1277960 | tf_op jit(solution)/shard_map/ppermute | solution.py:75
  53.7 23.7 %collective-permute-start.13 = (bf16[64,3328]{1,0:T(8,128)(2,1)S(1)}, bf16[64,3328]{1,0:T(8,128)(2,1)S(1)}, u32[]{:S(2)}, u32[]{:S(2)}) collective-permute-start(bf16[64,3328]{1,0:T(8,128)(2,1)S(1)} %collective-permute-done.11.refs_1_), channel_id=1, source_target_pairs={{0,4},{4,0},{8,12},{12,8},{1,5},{5,1},{9,13},{13,9},{2,6},{6,2},{1... | collective-permute-start | bytes 1277960 | tf_op jit(solution)/shard_map/ppermute | solution.py:75
  65.0 11.9 %collective-permute-start.19 = (bf16[64,2048]{1,0:T(8,128)(2,1)S(1)}, bf16[64,2048]{1,0:T(8,128)(2,1)S(1)}, u32[]{:S(2)}, u32[]{:S(2)}) collective-permute-start(bf16[64,2048]{1,0:T(8,128)(2,1)S(1)} %collective-permute-done.2.refs_4_), channel_id=1, source_target_pairs={{0,16},{16,0},{1,17},{17,1},{2,18},{18,2},{3,19},{19,3},{4,20},{20... | collective-permute-start | bytes 786440 | tf_op jit(solution)/shard_map/ppermute | solution.py:75
  65.5 15.4 %collective-permute-start.17 = (bf16[64,3328]{1,0:T(8,128)(2,1)S(1)}, bf16[64,3328]{1,0:T(8,128)(2,1)S(1)}, u32[]{:S(2)}, u32[]{:S(2)}) collective-permute-start(bf16[64,3328]{1,0:T(8,128)(2,1)S(1)} %collective-permute-done.15.refs_5_), channel_id=1, source_target_pairs={{0,4},{4,0},{8,12},{12,8},{1,5},{5,1},{9,13},{13,9},{2,6},{6,2},{1... | collective-permute-start | bytes 1277960 | tf_op jit(solution)/shard_map/ppermute | solution.py:75
  76.9 14.1 %collective-permute-start.4 = (bf16[64,1536]{1,0:T(8,128)(2,1)S(1)}, bf16[64,1536]{1,0:T(8,128)(2,1)S(1)}, u32[]{:S(2)}, u32[]{:S(2)}) collective-permute-start(bf16[64,1536]{1,0:T(8,128)(2,1)S(1)} %fusion.6), channel_id=1, source_target_pairs={{0,8},{4,12},{8,0},{12,4},{1,9},{5,13},{9,1},{13,5},{2,10},{6,14},... | collective-permute-start | bytes 589832 | tf_op jit(solution)/shard_map/ppermute | solution.py:75
  77.4 13.8 %collective-permute-start.6 = (bf16[64,1664]{1,0:T(8,128)(2,1)S(1)}, bf16[64,1664]{1,0:T(8,128)(2,1)S(1)}, u32[]{:S(2)}, u32[]{:S(2)}) collective-permute-start(bf16[64,1664]{1,0:T(8,128)(2,1)S(1)} %fusion.2), channel_id=1, source_target_pairs={{0,8},{4,12},{8,0},{12,4},{1,9},{5,13},{9,1},{13,5},{2,10},{6,14},... | collective-permute-start | bytes 638984 | tf_op jit(solution)/shard_map/ppermute | solution.py:75
  78.9 14.9 %collective-permute-start.8 = (bf16[64,1664]{1,0:T(8,128)(2,1)S(1)}, bf16[64,1664]{1,0:T(8,128)(2,1)S(1)}, u32[]{:S(2)}, u32[]{:S(2)}) collective-permute-start(bf16[64,1664]{1,0:T(8,128)(2,1)S(1)} %fusion.3), channel_id=1, source_target_pairs={{0,8},{4,12},{8,0},{12,4},{1,9},{5,13},{9,1},{13,5},{2,10},{6,14},... | collective-permute-start | bytes 638984 | tf_op jit(solution)/shard_map/ppermute | solution.py:75
  79.4 17.9 %collective-permute-start.10 = (bf16[64,1792]{1,0:T(8,128)(2,1)S(1)}, bf16[64,1792]{1,0:T(8,128)(2,1)S(1)}, u32[]{:S(2)}, u32[]{:S(2)}) collective-permute-start(bf16[64,1792]{1,0:T(8,128)(2,1)S(1)} %fusion), channel_id=1, source_target_pairs={{0,8},{4,12},{8,0},{12,4},{1,9},{5,13},{9,1},{13,5},{2,10},{6,14},... | collective-permute-start | bytes 688136 | tf_op jit(solution)/shard_map/ppermute | solution.py:75

commit v2 on v1

--- a/solution.py
+++ b/solution.py
@@ -1,4 +1,5 @@
 import functools
+import math
 
 import jax
 import jax.numpy as jnp
@@ -64,10 +65,8 @@
 
 def decode(code, scale):
     wide = code.astype(jnp.float32)
-    half = lax.rsqrt(jnp.maximum(jnp.abs(wide), 2.0**-126))
-    fourth = lax.rsqrt(half)
-    root = fourth * lax.rsqrt(fourth) * (1.0 / scale)
-    return jnp.where(wide < 0, -root, jnp.where(wide > 0, root, 0.0))
+    root = jnp.exp(jnp.log(jnp.abs(wide)) * (1.0 / POWER) - math.log(scale))
+    return jnp.where(wide < 0, -root, root)
 
 
 def swap(x, axis, mask):

time: 99 us -> 99 us (level)
  no operation moved by 1% of the time
where the time goes in v2:
time: 99 us; the launch traced here: 98.8 us
  waiting for transfers between devices  36.8 us (37%)
  Pallas kernels  33.3 us (34%)
  starting transfers between devices  19.9 us (20%)
  local copies, waits for them, and re-layouts  7.18 us (7%)
  between operations  1.02 us (1%)
    ppermute x20, waiting for transfers between devices, swap(): return lax.ppermute(x, axis, [(i, i ^ mask) for i in range(n)])  36.8 us
    ppermute x20, starting transfers between devices, swap(): return lax.ppermute(x, axis, [(i, i ^ mask) for i in range(n)])  19.9 us
    pallas_call x3, Pallas kernels, load(): pl.pallas_call(functools.partial(load_kernel, spans), in_specs=[pl.BlockS...  13.1 us
    pallas_call x1, Pallas kernels, weight_product(): pl.pallas_call(functools.partial(weight_kernel, len(hidden), pieces), in_...  10 us
    pallas_call x4, Pallas kernels, product(): pl.pallas_call(functools.partial(product_kernel, len(blocks), spans), in_...  8.65 us
    unnamed x14, local copies, waits for them, and re-layouts  7.11 us
  transfers between devices with their start and end apart: 20, of which 6 were waited for; matrix products, arithmetic and copies ran while one was open for 1% of the time, Pallas kernels for 30%

profile of v2, /device:TPU:0, one launch (start us, length us, event | category | flops | bytes accessed | tf_op | source)
XLA Modules:
  0.0 98.8 jit_solution(14145503212933154062)
XLA Ops:
  0.6 5.1 %collective-permute-start.1 = (bf16[64,2048]{1,0:T(8,128)(2,1)}, bf16[64,2048]{1,0:T(8,128)(2,1)S(1)}, u32[]{:S(2)}, u32[]{:S(2)}) collective-permute-start(bf16[64,2048]{1,0:T(8,128)(2,1)} %refs_1_.1), channel_id=1, source_target_pairs={{0,3},{1,2},{2,1},{3,0},{4,7},{5,6},{6,5},{7,4},{8,11},{9,10},{10,... | collective-permute-start | bytes 786440 | tf_op jit(solution)/shard_map/ppermute | solution.py:74
  5.8 7.5 %collective-permute-done.1.refs_3_ = bf16[64,2048]{1,0:T(8,128)(2,1)S(1)} collective-permute-done((bf16[64,2048]{1,0:T(8,128)(2,1)}, bf16[64,2048]{1,0:T(8,128)(2,1)S(1)}, u32[]{:S(2)}, u32[]{:S(2)}) %collective-permute-start.1) | collective-permute-done | bytes 262176 | tf_op jit(solution)/shard_map/ppermute | solution.py:74
  13.2 4.4 %collective-permute-start.2 = (bf16[64,2048]{1,0:T(8,128)(2,1)S(1)}, bf16[64,2048]{1,0:T(8,128)(2,1)S(1)}, u32[]{:S(2)}, u32[]{:S(2)}) collective-permute-start(bf16[64,2048]{1,0:T(8,128)(2,1)S(1)} %collective-permute-done.1.refs_3_), channel_id=1, source_target_pairs={{0,1},{1,0},{2,3},{3,2},{4,5},{5,4},{6,7},{7,6},{8,9},{9,8},{10,11... | collective-permute-start | bytes 786440 | tf_op jit(solution)/shard_map/ppermute | solution.py:74
  17.7 4.2 %shard_map.50.refs_5_.refs_1_ = bf16[2176,2048]{1,0:T(8,128)(2,1)S(1)} custom-call(s32[4]{0:T(128)S(1)} %pad_add_fusion.at.refs_0_, bf16[6656,2048]{1,0:T(8,128)(2,1)} %w.5), custom_call_target="tpu_custom_call" | custom-call | bytes 8912896 | tf_op jit(solution)/shard_map/pallas_call | solution.py:103
  21.9 3.6 %copy-done = bf16[2176,2048]{1,0:T(8,128)(2,1)} copy-done((bf16[2176,2048]{1,0:T(8,128)(2,1)}, bf16[2176,2048]{1,0:T(8,128)(2,1)S(1)}, u32[]{:S(2)}) %copy-start) | copy-done | bytes 8912920
  25.5 3.5 %copy-done.1 = bf16[2176,2048]{1,0:T(8,128)(2,1)S(1)} copy-done((bf16[2176,2048]{1,0:T(8,128)(2,1)S(1)}, bf16[2176,2048]{1,0:T(8,128)(2,1)}, u32[]{:S(2)}) %copy-start.1) | copy-done | bytes 8912920
  29.0 2.4 %shard_map.51 = (f32[128,1536]{1,0:T(8,128)S(1)}, f32[128,1536]{1,0:T(8,128)S(1)}, bf16[256,2048]{1,0:T(8,128)(2,1)S(1)}) custom-call(s32[4]{0:T(128)S(1)} %pad_add_fusion.at.refs_0_, bf16[64,2048]{1,0:T(8,128)(2,1)S(1)} %copy-done.2, bf16[64,2048]{1,0:T(8,128)(2,1)S(1)} %collective-permute-done.refs_2_, ...), custom_call_target="tpu_custom_call" | custom-call | flops 1610612736 | bytes 6291456 | tf_op jit(solution)/shard_map/pallas_call | solution.py:145
  31.5 1.6 %collective-permute-start.11 = (bf16[64,3328]{1,0:T(8,128)(2,1)S(1)}, bf16[64,3328]{1,0:T(8,128)(2,1)S(1)}, u32[]{:S(2)}, u32[]{:S(2)}) collective-permute-start(bf16[64,3328]{1,0:T(8,128)(2,1)S(1)} %get-tuple-element.21.refs_0_), channel_id=1, source_target_pairs={{0,8},{4,12},{8,0},{12,4},{1,9},{5,13},{9,1},{13,5},{2,10},{6,14},... | collective-permute-start | bytes 1277960 | tf_op jit(solution)/shard_map/ppermute | solution.py:74
  33.1 0.2 collective-permute-start.12
  33.3 1.5 %collective-permute-start.14 = (bf16[64,3328]{1,0:T(8,128)(2,1)S(1)}, bf16[64,3328]{1,0:T(8,128)(2,1)S(1)}, u32[]{:S(2)}, u32[]{:S(2)}) collective-permute-start(bf16[64,3328]{1,0:T(8,128)(2,1)S(1)} %get-tuple-element.20), channel_id=1, source_target_pairs={{0,16},{16,0},{1,17},{17,1},{2,18},{18,2},{3,19},{19,3},{4,20},{20... | collective-permute-start | bytes 1277960 | tf_op jit(solution)/shard_map/ppermute | solution.py:74
  34.8 4.4 %shard_map.53.refs_2_.refs_1_ = bf16[2176,2048]{1,0:T(8,128)(2,1)S(1)} custom-call(s32[4]{0:T(128)S(1)} %pad_add_fusion.at.refs_0_, bf16[6656,2048]{1,0:T(8,128)(2,1)} %w.5), custom_call_target="tpu_custom_call" | custom-call | bytes 8912896 | tf_op jit(solution)/shard_map/pallas_call | solution.py:103
  39.3 4.5 %shard_map.55.refs_2_.refs_1_ = bf16[2304,2048]{1,0:T(8,128)(2,1)S(1)} custom-call(s32[4]{0:T(128)S(1)} %pad_add_fusion.at.refs_0_, bf16[6656,2048]{1,0:T(8,128)(2,1)} %w.5), custom_call_target="tpu_custom_call" | custom-call | bytes 9437184 | tf_op jit(solution)/shard_map/pallas_call | solution.py:103
  43.9 2.1 %shard_map.54 = (f32[128,1664]{1,0:T(8,128)S(1)}, f32[128,1664]{1,0:T(8,128)S(1)}) custom-call(bf16[256,2048]{1,0:T(8,128)(2,1)S(1)} %get-tuple-element.13.refs_0_.refs_8_, bf16[2176,2048]{1,0:T(8,128)(2,1)S(1)} %bitcast.5, bf16[2176,2048]{1,0:T(8,128)(2,1)S(1)} %shard_map.53.refs_2_.refs_1_), custom_call_target="tpu_custom_call" | custom-call | flops 1744830464 | bytes 6815744 | tf_op jit(solution)/shard_map/pallas_call | solution.py:145
  46.1 2.1 %shard_map.56 = (f32[128,1664]{1,0:T(8,128)S(1)}, f32[128,1664]{1,0:T(8,128)S(1)}) custom-call(bf16[256,2048]{1,0:T(8,128)(2,1)S(1)} %get-tuple-element.13.refs_0_.refs_8_, bf16[2176,2048]{1,0:T(8,128)(2,1)S(1)} %shard_map.53.refs_2_.refs_1_, bf16[2304,2048]{1,0:T(8,128)(2,1)S(1)} %shard_map.55.refs_2_.refs_1_), custom_call_target="tpu_custom_call" | custom-call | flops 1744830464 | bytes 6815744 | tf_op jit(solution)/shard_map/pallas_call | solution.py:145
  48.2 2.1 %shard_map.57 = (f32[128,1792]{1,0:T(8,128)S(1)}, f32[128,1792]{1,0:T(8,128)S(1)}) custom-call(bf16[256,2048]{1,0:T(8,128)(2,1)S(1)} %get-tuple-element.13.refs_0_.refs_8_, bf16[2304,2048]{1,0:T(8,128)(2,1)S(1)} %shard_map.55.refs_2_.refs_1_), custom_call_target="tpu_custom_call" | custom-call | flops 1879048192 | bytes 7340032 | tf_op jit(solution)/shard_map/pallas_call | solution.py:145
  50.3 0.5 collective-permute-start.7
  51.2 0.6 collective-permute-start.18
  51.8 1.1 %collective-permute-done.7.refs_5_ = f32[128,1664]{1,0:T(8,128)S(1)} collective-permute-done((f32[128,1664]{1,0:T(8,128)S(1)}, f32[128,1664]{1,0:T(8,128)S(1)}, u32[]{:S(2)}, u32[]{:S(2)}) %collective-permute-start.7) | collective-permute-done | bytes 852000 | tf_op jit(solution)/shard_map/ppermute | solution.py:74
  52.9 0.5 collective-permute-start.15
  53.7 0.4 collective-permute-start.13
  54.1 10.8 %collective-permute-done.15.refs_5_ = bf16[64,3328]{1,0:T(8,128)(2,1)S(1)} collective-permute-done((bf16[64,3328]{1,0:T(8,128)(2,1)S(1)}, bf16[64,3328]{1,0:T(8,128)(2,1)S(1)}, u32[]{:S(2)}, u32[]{:S(2)}) %collective-permute-start.15) | collective-permute-done | bytes 426016 | tf_op jit(solution)/shard_map/ppermute | solution.py:74
  65.0 0.5 collective-permute-start.19
  65.6 11.2 %collective-permute-done.19.refs_10_ = bf16[64,2048]{1,0:T(8,128)(2,1)S(1)} collective-permute-done((bf16[64,2048]{1,0:T(8,128)(2,1)S(1)}, bf16[64,2048]{1,0:T(8,128)(2,1)S(1)}, u32[]{:S(2)}, u32[]{:S(2)}) %collective-permute-start.19) | collective-permute-done | bytes 262176 | tf_op jit(solution)/shard_map/ppermute | solution.py:74
  76.9 0.5 collective-permute-start.4
  77.4 1.5 %collective-permute-start.6 = (bf16[64,1664]{1,0:T(8,128)(2,1)S(1)}, bf16[64,1664]{1,0:T(8,128)(2,1)S(1)}, u32[]{:S(2)}, u32[]{:S(2)}) collective-permute-start(bf16[64,1664]{1,0:T(8,128)(2,1)S(1)} %fusion.2), channel_id=1, source_target_pairs={{0,8},{4,12},{8,0},{12,4},{1,9},{5,13},{9,1},{13,5},{2,10},{6,14},... | collective-permute-start | bytes 638984 | tf_op jit(solution)/shard_map/ppermute | solution.py:74
  78.9 0.5 collective-permute-start.8
  79.4 1.5 %collective-permute-start.10 = (bf16[64,1792]{1,0:T(8,128)(2,1)S(1)}, bf16[64,1792]{1,0:T(8,128)(2,1)S(1)}, u32[]{:S(2)}, u32[]{:S(2)}) collective-permute-start(bf16[64,1792]{1,0:T(8,128)(2,1)S(1)} %fusion), channel_id=1, source_target_pairs={{0,8},{4,12},{8,0},{12,4},{1,9},{5,13},{9,1},{13,5},{2,10},{6,14},... | collective-permute-start | bytes 688136 | tf_op jit(solution)/shard_map/ppermute | solution.py:74
  80.9 10.0 %shard_map.59 = bf16[3328,2048]{1,0:T(8,128)(2,1)} custom-call(s32[4]{0:T(128)S(1)} %pad_add_fusion.at.refs_0_, bf16[64,3328]{1,0:T(8,128)(2,1)S(1)} %get-tuple-element.21.refs_0_, bf16[64,3328]{1,0:T(8,128)(2,1)S(1)} %collective-permute-done.11.refs_1_, bf16[64,3328]{1,0:T(8,128)(2,1)S(1)} %collective-permute-done.12.refs_2_, ...), custom_call_target="tpu_custom_call" | custom-call | flops 6979321856 | bytes 13631488 | tf_op jit(solution)/shard_map/pallas_call | solution.py:267
  91.0 0.2 shard_map.52.refs_0_
  91.2 2.6 %collective-permute-done.8.refs_6_ = bf16[64,1664]{1,0:T(8,128)(2,1)S(1)} collective-permute-done((bf16[64,1664]{1,0:T(8,128)(2,1)S(1)}, bf16[64,1664]{1,0:T(8,128)(2,1)S(1)}, u32[]{:S(2)}, u32[]{:S(2)}) %collective-permute-start.8) | collective-permute-done | bytes 213024 | tf_op jit(solution)/shard_map/ppermute | solution.py:74
  93.8 3.6 %collective-permute-done.10.refs_9_ = bf16[64,1792]{1,0:T(8,128)(2,1)S(1)} collective-permute-done((bf16[64,1792]{1,0:T(8,128)(2,1)S(1)}, bf16[64,1792]{1,0:T(8,128)(2,1)S(1)}, u32[]{:S(2)}, u32[]{:S(2)}) %collective-permute-start.10) | collective-permute-done | bytes 229408 | tf_op jit(solution)/shard_map/ppermute | solution.py:74
  97.3 1.3 %shard_map.58 = bf16[64,6656]{1,0:T(8,128)(2,1)} custom-call(bf16[64,1536]{1,0:T(8,128)(2,1)S(1)} %shard_map.52.refs_0_, f32[128,1664]{1,0:T(8,128)S(1)} %get-tuple-element.14.refs_1_, f32[128,1664]{1,0:T(8,128)S(1)} %collective-permute-done.5.refs_2_, bf16[64,1664]{1,0:T(8,128)(2,1)S(1)} %collective-permute-done.6.refs_3_, ...), custom_call_target="tpu_custom_call" | custom-call | flops 8519680 | bytes 5963776 | tf_op jit(solution)/shard_map/pallas_call | solution.py:196
  (40 shorter events, 1.2 us)
Async XLA Ops:
  0.6 12.6 %collective-permute-start.1 = (bf16[64,2048]{1,0:T(8,128)(2,1)}, bf16[64,2048]{1,0:T(8,128)(2,1)S(1)}, u32[]{:S(2)}, u32[]{:S(2)}) collective-permute-start(bf16[64,2048]{1,0:T(8,128)(2,1)} %refs_1_.1), channel_id=1, source_target_pairs={{0,3},{1,2},{2,1},{3,0},{4,7},{5,6},{6,5},{7,4},{8,11},{9,10},{10,... | collective-permute-start | bytes 786440 | tf_op jit(solution)/shard_map/ppermute | solution.py:74
  5.8 19.7 %collective-permute-start = (bf16[64,2048]{1,0:T(8,128)(2,1)}, bf16[64,2048]{1,0:T(8,128)(2,1)S(1)}, u32[]{:S(2)}, u32[]{:S(2)}) collective-permute-start(bf16[64,2048]{1,0:T(8,128)(2,1)} %refs_1_.1), channel_id=1, source_target_pairs={{0,1},{1,0},{2,3},{3,2},{4,5},{5,4},{6,7},{7,6},{8,9},{9,8},{10,11... | collective-permute-start | bytes 786440 | tf_op jit(solution)/shard_map/ppermute | solution.py:74
  13.2 12.2 %collective-permute-start.2 = (bf16[64,2048]{1,0:T(8,128)(2,1)S(1)}, bf16[64,2048]{1,0:T(8,128)(2,1)S(1)}, u32[]{:S(2)}, u32[]{:S(2)}) collective-permute-start(bf16[64,2048]{1,0:T(8,128)(2,1)S(1)} %collective-permute-done.1.refs_3_), channel_id=1, source_target_pairs={{0,1},{1,0},{2,3},{3,2},{4,5},{5,4},{6,7},{7,6},{8,9},{9,8},{10,11... | collective-permute-start | bytes 786440 | tf_op jit(solution)/shard_map/ppermute | solution.py:74
  17.7 7.8 %copy-start.2 = (bf16[64,2048]{1,0:T(8,128)(2,1)S(1)}, bf16[64,2048]{1,0:T(8,128)(2,1)}, u32[]{:S(2)}) copy-start(bf16[64,2048]{1,0:T(8,128)(2,1)} %refs_1_.1) | copy-start | bytes 786436
  17.7 13.8 %copy-start.3 = (bf16[64,6656]{1,0:T(8,128)(2,1)S(1)}, bf16[64,6656]{1,0:T(8,128)(2,1)}, u32[]{:S(2)}) copy-start(bf16[64,6656]{1,0:T(8,128)(2,1)} %param.4) | copy-start | bytes 2555908
  21.9 3.6 %copy-start = (bf16[2176,2048]{1,0:T(8,128)(2,1)}, bf16[2176,2048]{1,0:T(8,128)(2,1)S(1)}, u32[]{:S(2)}) copy-start(bf16[2176,2048]{1,0:T(8,128)(2,1)S(1)} %shard_map.50.refs_5_.refs_1_) | copy-start | bytes 26738692
  25.5 3.5 %copy-start.1 = (bf16[2176,2048]{1,0:T(8,128)(2,1)S(1)}, bf16[2176,2048]{1,0:T(8,128)(2,1)}, u32[]{:S(2)}) copy-start(bf16[2176,2048]{1,0:T(8,128)(2,1)} %copy-done) | copy-start | bytes 26738692
  31.4 18.9 %collective-permute-start.3 = (f32[128,1536]{1,0:T(8,128)S(1)}, f32[128,1536]{1,0:T(8,128)S(1)}, u32[]{:S(2)}, u32[]{:S(2)}) collective-permute-start(f32[128,1536]{1,0:T(8,128)S(1)} %get-tuple-element.12), channel_id=1, source_target_pairs={{0,4},{4,0},{8,12},{12,8},{1,5},{5,1},{9,13},{13,9},{2,6},{6,2},{1... | collective-permute-start | bytes 2359304 | tf_op jit(solution)/shard_map/ppermute | solution.py:74
  31.5 22.0 %collective-permute-start.11 = (bf16[64,3328]{1,0:T(8,128)(2,1)S(1)}, bf16[64,3328]{1,0:T(8,128)(2,1)S(1)}, u32[]{:S(2)}, u32[]{:S(2)}) collective-permute-start(bf16[64,3328]{1,0:T(8,128)(2,1)S(1)} %get-tuple-element.21.refs_0_), channel_id=1, source_target_pairs={{0,8},{4,12},{8,0},{12,4},{1,9},{5,13},{9,1},{13,5},{2,10},{6,14},... | collective-permute-start | bytes 1277960 | tf_op jit(solution)/shard_map/ppermute | solution.py:74
  33.1 20.6 %collective-permute-start.12 = (bf16[64,3328]{1,0:T(8,128)(2,1)S(1)}, bf16[64,3328]{1,0:T(8,128)(2,1)S(1)}, u32[]{:S(2)}, u32[]{:S(2)}) collective-permute-start(bf16[64,3328]{1,0:T(8,128)(2,1)S(1)} %get-tuple-element.21.refs_0_), channel_id=1, source_target_pairs={{0,4},{4,0},{8,12},{12,8},{1,5},{5,1},{9,13},{13,9},{2,6},{6,2},{1... | collective-permute-start | bytes 1277960 | tf_op jit(solution)/shard_map/ppermute | solution.py:74
  33.3 17.9 %collective-permute-start.14 = (bf16[64,3328]{1,0:T(8,128)(2,1)S(1)}, bf16[64,3328]{1,0:T(8,128)(2,1)S(1)}, u32[]{:S(2)}, u32[]{:S(2)}) collective-permute-start(bf16[64,3328]{1,0:T(8,128)(2,1)S(1)} %get-tuple-element.20), channel_id=1, source_target_pairs={{0,16},{16,0},{1,17},{17,1},{2,18},{18,2},{3,19},{19,3},{4,20},{20... | collective-permute-start | bytes 1277960 | tf_op jit(solution)/shard_map/ppermute | solution.py:74
  34.8 9.0 %slice-start = ((s8[8912896]{0:T(1024)(128)(4,1)}), s8[4194304]{0:T(1024)(128)(4,1)S(1)}, s32[]{:S(2)}) async-start(s8[8912896]{0:T(1024)(128)(4,1)} %bitcast.4), calls=%async_computation | async-start | bytes 8388608
  34.8 9.0 %slice-start.1 = ((s8[8912896]{0:T(1024)(128)(4,1)}), s8[4194304]{0:T(1024)(128)(4,1)S(1)}, s32[]{:S(2)}) async-start(s8[8912896]{0:T(1024)(128)(4,1)} %bitcast.4), calls=%async_computation.1 | async-start | bytes 8388608
  39.3 4.6 %slice-start.2 = ((s8[8912896]{0:T(1024)(128)(4,1)}), s8[524288]{0:T(1024)(128)(4,1)S(1)}, s32[]{:S(2)}) async-start(s8[8912896]{0:T(1024)(128)(4,1)} %bitcast.4), calls=%async_computation.2 | async-start | bytes 1048576
  46.0 5.0 %collective-permute-start.5 = (f32[128,1664]{1,0:T(8,128)S(1)}, f32[128,1664]{1,0:T(8,128)S(1)}, u32[]{:S(2)}, u32[]{:S(2)}) collective-permute-start(f32[128,1664]{1,0:T(8,128)S(1)} %get-tuple-element.15), channel_id=1, source_target_pairs={{0,4},{4,0},{8,12},{12,8},{1,5},{5,1},{9,13},{13,9},{2,6},{6,2},{1... | collective-permute-start | bytes 2555912 | tf_op jit(solution)/shard_map/ppermute | solution.py:74
  50.3 2.5 %collective-permute-start.7 = (f32[128,1664]{1,0:T(8,128)S(1)}, f32[128,1664]{1,0:T(8,128)S(1)}, u32[]{:S(2)}, u32[]{:S(2)}) collective-permute-start(f32[128,1664]{1,0:T(8,128)S(1)} %get-tuple-element.17), channel_id=1, source_target_pairs={{0,4},{4,0},{8,12},{12,8},{1,5},{5,1},{9,13},{13,9},{2,6},{6,2},{1... | collective-permute-start | bytes 2555912 | tf_op jit(solution)/shard_map/ppermute | solution.py:74
  51.0 14.5 %collective-permute-start.9 = (f32[128,1792]{1,0:T(8,128)S(1)}, f32[128,1792]{1,0:T(8,128)S(1)}, u32[]{:S(2)}, u32[]{:S(2)}) collective-permute-start(f32[128,1792]{1,0:T(8,128)S(1)} %get-tuple-element.19), channel_id=1, source_target_pairs={{0,4},{4,0},{8,12},{12,8},{1,5},{5,1},{9,13},{13,9},{2,6},{6,2},{1... | collective-permute-start | bytes 2752520 | tf_op jit(solution)/shard_map/ppermute | solution.py:74
  51.2 28.2 %collective-permute-start.18 = (bf16[192,2048]{1,0:T(8,128)(2,1)S(1)}, bf16[192,2048]{1,0:T(8,128)(2,1)S(1)}, u32[]{:S(2)}, u32[]{:S(2)}) collective-permute-start(bf16[192,2048]{1,0:T(8,128)(2,1)S(1)} %pad_maximum_fusion), channel_id=1, source_target_pairs={{0,16},{16,0},{1,17},{17,1},{2,18},{18,2},{3,19},{19,3},{4,20},{20... | collective-permute-start | bytes 2359304 | tf_op jit(solution)/shard_map/ppermute | solution.py:74
  52.9 12.1 %collective-permute-start.15 = (bf16[64,3328]{1,0:T(8,128)(2,1)S(1)}, bf16[64,3328]{1,0:T(8,128)(2,1)S(1)}, u32[]{:S(2)}, u32[]{:S(2)}) collective-permute-start(bf16[64,3328]{1,0:T(8,128)(2,1)S(1)} %collective-permute-done.14.refs_4_), channel_id=1, source_target_pairs={{0,8},{4,12},{8,0},{12,4},{1,9},{5,13},{9,1},{13,5},{2,10},{6,14},... | collective-permute-start | bytes 1277960 | tf_op jit(solution)/shard_map/ppermute | solution.py:74
  53.6 25.3 %collective-permute-start.16 = (bf16[64,3328]{1,0:T(8,128)(2,1)S(1)}, bf16[64,3328]{1,0:T(8,128)(2,1)S(1)}, u32[]{:S(2)}, u32[]{:S(2)}) collective-permute-start(bf16[64,3328]{1,0:T(8,128)(2,1)S(1)} %collective-permute-done.14.refs_4_), channel_id=1, source_target_pairs={{0,4},{4,0},{8,12},{12,8},{1,5},{5,1},{9,13},{13,9},{2,6},{6,2},{1... | collective-permute-start | bytes 1277960 | tf_op jit(solution)/shard_map/ppermute | solution.py:74
  53.7 23.7 %collective-permute-start.13 = (bf16[64,3328]{1,0:T(8,128)(2,1)S(1)}, bf16[64,3328]{1,0:T(8,128)(2,1)S(1)}, u32[]{:S(2)}, u32[]{:S(2)}) collective-permute-start(bf16[64,3328]{1,0:T(8,128)(2,1)S(1)} %collective-permute-done.11.refs_1_), channel_id=1, source_target_pairs={{0,4},{4,0},{8,12},{12,8},{1,5},{5,1},{9,13},{13,9},{2,6},{6,2},{1... | collective-permute-start | bytes 1277960 | tf_op jit(solution)/shard_map/ppermute | solution.py:74
  65.0 11.9 %collective-permute-start.19 = (bf16[64,2048]{1,0:T(8,128)(2,1)S(1)}, bf16[64,2048]{1,0:T(8,128)(2,1)S(1)}, u32[]{:S(2)}, u32[]{:S(2)}) collective-permute-start(bf16[64,2048]{1,0:T(8,128)(2,1)S(1)} %collective-permute-done.2.refs_4_), channel_id=1, source_target_pairs={{0,16},{16,0},{1,17},{17,1},{2,18},{18,2},{3,19},{19,3},{4,20},{20... | collective-permute-start | bytes 786440 | tf_op jit(solution)/shard_map/ppermute | solution.py:74
  65.5 15.4 %collective-permute-start.17 = (bf16[64,3328]{1,0:T(8,128)(2,1)S(1)}, bf16[64,3328]{1,0:T(8,128)(2,1)S(1)}, u32[]{:S(2)}, u32[]{:S(2)}) collective-permute-start(bf16[64,3328]{1,0:T(8,128)(2,1)S(1)} %collective-permute-done.15.refs_5_), channel_id=1, source_target_pairs={{0,4},{4,0},{8,12},{12,8},{1,5},{5,1},{9,13},{13,9},{2,6},{6,2},{1... | collective-permute-start | bytes 1277960 | tf_op jit(solution)/shard_map/ppermute | solution.py:74
  76.9 14.1 %collective-permute-start.4 = (bf16[64,1536]{1,0:T(8,128)(2,1)S(1)}, bf16[64,1536]{1,0:T(8,128)(2,1)S(1)}, u32[]{:S(2)}, u32[]{:S(2)}) collective-permute-start(bf16[64,1536]{1,0:T(8,128)(2,1)S(1)} %fusion.6), channel_id=1, source_target_pairs={{0,8},{4,12},{8,0},{12,4},{1,9},{5,13},{9,1},{13,5},{2,10},{6,14},... | collective-permute-start | bytes 589832 | tf_op jit(solution)/shard_map/ppermute | solution.py:74
  77.4 13.8 %collective-permute-start.6 = (bf16[64,1664]{1,0:T(8,128)(2,1)S(1)}, bf16[64,1664]{1,0:T(8,128)(2,1)S(1)}, u32[]{:S(2)}, u32[]{:S(2)}) collective-permute-start(bf16[64,1664]{1,0:T(8,128)(2,1)S(1)} %fusion.2), channel_id=1, source_target_pairs={{0,8},{4,12},{8,0},{12,4},{1,9},{5,13},{9,1},{13,5},{2,10},{6,14},... | collective-permute-start | bytes 638984 | tf_op jit(solution)/shard_map/ppermute | solution.py:74
  78.9 14.9 %collective-permute-start.8 = (bf16[64,1664]{1,0:T(8,128)(2,1)S(1)}, bf16[64,1664]{1,0:T(8,128)(2,1)S(1)}, u32[]{:S(2)}, u32[]{:S(2)}) collective-permute-start(bf16[64,1664]{1,0:T(8,128)(2,1)S(1)} %fusion.3), channel_id=1, source_target_pairs={{0,8},{4,12},{8,0},{12,4},{1,9},{5,13},{9,1},{13,5},{2,10},{6,14},... | collective-permute-start | bytes 638984 | tf_op jit(solution)/shard_map/ppermute | solution.py:74
  79.4 17.9 %collective-permute-start.10 = (bf16[64,1792]{1,0:T(8,128)(2,1)S(1)}, bf16[64,1792]{1,0:T(8,128)(2,1)S(1)}, u32[]{:S(2)}, u32[]{:S(2)}) collective-permute-start(bf16[64,1792]{1,0:T(8,128)(2,1)S(1)} %fusion), channel_id=1, source_target_pairs={{0,8},{4,12},{8,0},{12,4},{1,9},{5,13},{9,1},{13,5},{2,10},{6,14},... | collective-permute-start | bytes 688136 | tf_op jit(solution)/shard_map/ppermute | solution.py:74
